TPU v7x, 128 devices: a whole 4x4x4 slice. The times are simulated.
128 devices in a mesh: sp: 32 (over x, z_hi, y), ch: 4 (over z_lo, core).
Axes of the slice: x: 4, y: 4, z: 4 (z_hi: 2, z_lo: 2; z = z_hi * 2 + z_lo), core: 2. Of those that a mesh axis runs over, the one named last changes fastest.
Arguments:
- x_in: bfloat16 [256, 64, 128], P('ch', 'sp'), may hold values from -6 to 6
- gate_in: bfloat16 [256, 64, 128], P('ch', 'sp'), may hold values from -6 to 6
- conv_weight: float32 [256, 9], P('ch'), may hold values from -2 to 2
- conv_bias: float32 [256], P('ch'), may hold values from -0.5 to 0.5
- proj_weight: bfloat16 [4, 40, 256], P(None, None, 'ch'), may hold values from -0.375 to 0.375
- dt_weight: float32 [4, 256, 8], P(None, 'ch'), may hold values from -2 to 2
- dt_bias: float32 [4, 256], P(None, 'ch'), may hold values from -2 to 1
- decay_rate: float32 [4, 256, 16], P(None, 'ch'), may hold values from 0.0005 to 0.1
- skip_gain: float32 [4, 256], P(None, 'ch'), may hold values from 0.5 to 1.5
- norm_gain: float32 [256], P('ch'), may hold values from 0.5 to 1.5
- norm_bias: float32 [256], P('ch'), may hold values from -0.5 to 0.5
Outputs:
- mixed: bfloat16 [256, 64, 128], P('ch', 'sp')
All inputs are finite; a program needn't handle non-finite values.
Results may differ from a plain program's by a relative error of at most 0.014.
Values may be sent and summed in bfloat16 or wider, within the bound.
No kernel may reach another device: no remote copies, remote signals or barrier semaphores. Data moves between devices by JAX's collectives and lax.ppermute only.
A program may use at most 64 MiB of HBM per device.

v0:
```python
import math

import jax
import jax.numpy as jnp
from jax import lax
from jax.experimental import pallas as pl
from jax.experimental.pallas import tpu as pltpu
from jax.sharding import PartitionSpec as P

F32 = jnp.float32
BF16 = jnp.bfloat16
LANES = 128
EXACT = lax.Precision.HIGHEST
NEG_LOG2E = -1.0 / math.log(2.0)

PROJ_ROWS = 160
VEC_ROWS = 64
WBUF_ROWS = PROJ_ROWS + 2 * VEC_ROWS


def iota(shape, axis):
    return lax.broadcasted_iota(jnp.int32, shape, axis)


def dup_matrix(chans):
    return jnp.where(iota((chans, 2 * chans), 1) // 2 == iota((chans, 2 * chans), 0), 1.0, 0.0).astype(F32)


def dup_rows(value, dup):
    return jnp.dot(value, dup, preferred_element_type=F32, precision=EXACT)


def dup_cols(value, dup):
    return lax.dot_general(
        value, dup, (((0,), (0,)), ((), ())), preferred_element_type=F32, precision=EXACT
    )


def softplus(x):
    return jnp.maximum(x, 0.0) + jnp.log1p(jnp.exp(-jnp.abs(x)))


def silu(x):
    return x * jax.nn.sigmoid(x)


def roll(x, shift, axis):
    return pltpu.roll(x, shift % x.shape[axis], axis)


def prep_kernel(x_ref, cw_ref, cb_ref, pw_ref, dtw_ref, dtb_ref, rate_ref, skip_ref, send_ref, w_ref, scr, vec):
    turned = x_ref[...].astype(F32).T
    scr[pl.ds(12, LANES, stride=4), :] = turned
    scr[pl.ds(9, LANES, stride=4), :] = turned
    scr[pl.ds(6, LANES, stride=4), :] = turned
    scr[pl.ds(11, LANES, stride=4), :] = jnp.zeros((LANES, LANES), F32)
    scr[8:9, :] = jnp.zeros((1, LANES), F32)
    scr[8 + 4 * 127 + 2 : 8 + 4 * 127 + 3, :] = jnp.zeros((1, LANES), F32)
    send_ref[...] = scr[8 : 8 + 4 * LANES, :].astype(BF16)

    chans = cw_ref.shape[0]
    dup = dup_matrix(chans)
    dup_b = dup.astype(BF16)
    first = jnp.dot(
        jnp.concatenate([pw_ref[0].astype(F32), pw_ref[1].astype(F32)], axis=0).astype(BF16),
        dup_b,
        preferred_element_type=F32,
    )
    w_ref[0:80, :] = first.astype(BF16)
    third = pw_ref[2].astype(F32)
    fourth = pw_ref[3].astype(F32)
    rest = jnp.concatenate([third[0:8], fourth[0:8], third[8:40], fourth[8:40]], axis=0)
    w_ref[80:160, :] = jnp.dot(rest.astype(BF16), dup_b, preferred_element_type=F32).astype(BF16)

    vec[0:9, :] = dup_cols(cw_ref[...], dup)
    vec[9:10, :] = dup_rows(cb_ref[...], dup)
    vec[10:12, :] = dup_rows(dtb_ref[...], dup)[2:4]
    vec[12:14, :] = dup_rows(skip_ref[...], dup)[2:4]
    vec[14:16, :] = jnp.zeros((2, LANES), F32)
    vec[16:24, :] = dup_cols(dtw_ref[2], dup)
    vec[24:32, :] = dup_cols(dtw_ref[3], dup)
    vec[32:48, :] = dup_cols(rate_ref[2], dup)
    vec[48:64, :] = dup_cols(rate_ref[3], dup)
    whole = vec[...]
    high = whole.astype(BF16)
    w_ref[PROJ_ROWS : PROJ_ROWS + VEC_ROWS, :] = high
    w_ref[PROJ_ROWS + VEC_ROWS :, :] = (whole - high.astype(F32)).astype(BF16)


def scan_pair(steps, rates, delta_refs, drive_refs, b_at, c_at, y_refs, row_of):
    width = rates[0].shape[1]
    states = [jnp.zeros(rates[0].shape, F32) for _ in range(2)]
    for step in range(steps):
        for way in range(2):
            at = step if way == 0 else steps - 1 - step
            row = row_of(at)
            delta = delta_refs[way][row : row + 1, :]
            drive = drive_refs[way][row : row + 1, :]
            decay = jnp.exp2(delta * rates[way])
            states[way] = decay * states[way] + drive * b_at(way, at, width)
            y_refs[way][row : row + 1, :] = jnp.sum(
                c_at(way, at, width) * states[way], axis=0, keepdims=True
            )


def column_kernel(recv_ref, own_ref, w1_ref, w2_ref, w3_ref, send_ref, scr, wall, delta2, delta3, drive2, drive3, y2, y3):
    me = lax.axis_index("ch")
    slabs = LANES // 4
    wall[me] = own_ref[...]
    wall[me ^ 1] = w1_ref[...]
    wall[me ^ 2] = w2_ref[...]
    wall[me ^ 3] = w3_ref[...]

    scr[0:16, :] = jnp.zeros((16, LANES), F32)
    scr[16 + 512 : 32 + 512, :] = jnp.zeros((16, LANES), F32)
    scr[16 : 16 + 512, :] = recv_ref[...].astype(F32)

    even = iota((slabs, LANES), 1) % 2 == 0
    vecs = []
    conv = []
    for group in range(4):
        vec = wall[group, PROJ_ROWS : PROJ_ROWS + VEC_ROWS, :].astype(F32) + wall[
            group, PROJ_ROWS + VEC_ROWS :, :
        ].astype(F32)
        vecs.append(vec)
        total = jnp.zeros((slabs, LANES), F32) + vec[9:10, :]
        for side in range(3):
            base = 16 + 4 * group + side
            above = scr[pl.ds(base - 16, slabs, stride=16), :]
            here = scr[pl.ds(base, slabs, stride=16), :]
            below = scr[pl.ds(base + 16, slabs, stride=16), :]
            here_next = roll(here, -1, 1)
            here_prev = roll(here, 1, 1)
            up = jnp.where(even, roll(above, -1, 1), here_prev)
            down = jnp.where(even, here_next, roll(below, 1, 1))
            total = total + vec[side : side + 1, :] * up
            total = total + vec[3 + side : 4 + side, :] * here
            total = total + vec[6 + side : 7 + side, :] * down
        conv.append(silu(total).astype(BF16).astype(F32))

    evens = [jnp.where(even, conv[2 * p], roll(conv[2 * p + 1], 1, 1)) for p in range(2)]
    odds = [jnp.where(even, roll(conv[2 * p], -1, 1), conv[2 * p + 1]) for p in range(2)]
    values = jnp.concatenate(
        [jnp.concatenate(evens, axis=1), jnp.concatenate(odds, axis=1)], axis=0
    )
    values_b = values.astype(BF16)

    even_w = iota((WBUF_ROWS, LANES), 1) % 2 == 0
    weights = jnp.concatenate(
        [
            jnp.where(even_w, wall[2 * p].astype(F32), wall[2 * p + 1].astype(F32))
            for p in range(2)
        ],
        axis=1,
    )
    proj_w = weights[0:PROJ_ROWS].astype(BF16)
    vec = weights[PROJ_ROWS : PROJ_ROWS + VEC_ROWS] + weights[PROJ_ROWS + VEC_ROWS :]

    nt = (((1,), (1,)), ((), ()))
    proj = lax.dot_general(values_b, proj_w[0:128], nt, preferred_element_type=F32)
    proj = proj.astype(BF16).astype(F32)
    turned = lax.dot_general(proj_w[96:160], values_b, nt, preferred_element_type=F32)
    turned = turned.astype(BF16).astype(F32)

    low = lax.dot_general(values_b, proj_w[80:96], nt, preferred_element_type=F32)
    low = low.astype(BF16).astype(F32)
    dt_rows = vec[16:32]
    second_half = iota((16, 256), 0) >= 8
    for way, (delta_ref, drive_ref) in enumerate(((delta2, drive2), (delta3, drive3))):
        chosen = jnp.where(second_half == (way == 1), dt_rows, 0.0)
        delta = softplus(
            jnp.dot(low, chosen, preferred_element_type=F32, precision=EXACT)
            + vec[10 + way : 11 + way, :]
        )
        delta_ref[...] = delta
        drive_ref[...] = delta * values
    rates = [vec[32 + 16 * way : 48 + 16 * way] * NEG_LOG2E for way in range(2)]

    def row_of(at):
        return (at % 2) * slabs + at // 2

    def part(way, at, width, offset):
        column = row_of(at)
        first = 32 * way + offset
        return jnp.broadcast_to(turned[first : first + 16, column : column + 1], (16, width))

    scan_pair(
        2 * slabs,
        rates,
        (delta2, delta3),
        (drive2, drive3),
        lambda way, at, width: part(way, at, width, 0),
        lambda way, at, width: part(way, at, width, 16),
        (y2, y3),
        row_of,
    )

    y = y2[...] + y3[...] + (vec[12:13] + vec[13:14]) * values
    for group in range(4):
        pair = slice(LANES * (group // 2), LANES * (group // 2) + LANES)
        y_even = y[0:slabs, pair]
        y_odd = y[slabs:, pair]
        if group % 2 == 0:
            back = jnp.where(even, y_even, roll(y_odd, 1, 1))
        else:
            back = jnp.where(even, roll(y_even, -1, 1), y_odd)
        base = 4 * group
        scr[pl.ds(base, slabs, stride=16), :] = back
        scr[pl.ds(base + 1, slabs, stride=16), :] = conv[group]
        scr[pl.ds(base + 2, slabs, stride=16), :] = proj[0:slabs]
        scr[pl.ds(base + 3, slabs, stride=16), :] = proj[slabs:]
    send_ref[...] = scr[0:512, :].astype(BF16)


def row_kernel(recv_ref, dtw_ref, dtb_ref, rate_ref, skip_ref, comb_ref, sums_ref, scr, delta0, delta1, drive0, drive1, y0, y1):
    scr[...] = recv_ref[...].astype(F32)
    cols = LANES
    vertical = scr[pl.ds(0, cols, stride=4), :]
    values = scr[pl.ds(1, cols, stride=4), :]
    proj = [scr[pl.ds(2 + row, cols, stride=4), :] for row in range(2)]

    chans = dtw_ref.shape[1]
    dup = dup_matrix(chans)
    bias = dup_rows(dtb_ref[...], dup)
    skip = dup_rows(skip_ref[...], dup)
    lane_row = iota((8, LANES), 1) % 2
    rates = []
    for way, (delta_ref, drive_ref) in enumerate(((delta0, drive0), (delta1, drive1))):
        dt_rows = dup_cols(dtw_ref[way], dup)
        total = jnp.zeros((cols, LANES), F32) + bias[way : way + 1, :]
        for row in range(2):
            mine = jnp.where(lane_row == row, dt_rows, 0.0)
            parts = [mine, jnp.zeros((LANES - 40 * way - 8, LANES), F32)]
            if way:
                parts = [jnp.zeros((40 * way, LANES), F32)] + parts
            total = total + jnp.dot(
                proj[row], jnp.concatenate(parts, axis=0), preferred_element_type=F32, precision=EXACT
            )
        delta = softplus(total)
        delta_ref[...] = delta
        drive_ref[...] = delta * values
        rates.append(dup_cols(rate_ref[way], dup) * NEG_LOG2E)

    turned = [p.T for p in proj]
    even = iota((16, LANES), 1) % 2 == 0

    def part(way, at, width, offset):
        first = 40 * way + offset
        left = jnp.broadcast_to(turned[0][first : first + 16, at : at + 1], (16, width))
        right = jnp.broadcast_to(turned[1][first : first + 16, at : at + 1], (16, width))
        return jnp.where(even, left, right)

    scan_pair(
        cols,
        rates,
        (delta0, delta1),
        (drive0, drive1),
        lambda way, at, width: part(way, at, width, 8),
        lambda way, at, width: part(way, at, width, 24),
        (y0, y1),
        lambda at: at,
    )
    combined = y0[...] + y1[...] + (skip[0:1] + skip[1:2]) * values + vertical
    turned_back = combined.T
    comb_ref[...] = turned_back
    for index, value in enumerate((turned_back, turned_back * turned_back)):
        part_sum = value[0:8]
        for tile in range(1, LANES // 8):
            part_sum = part_sum + value[8 * tile : 8 * tile + 8]
        part_sum = part_sum + roll(part_sum, 4, 0)
        part_sum = part_sum + roll(part_sum, 2, 0)
        sums_ref[8 * index : 8 * index + 8, :] = part_sum


def norm_kernel(total_chans, comb_ref, s0_ref, s1_ref, s2_ref, s3_ref, gate_ref, gain_ref, bias_ref, out_ref):
    sums = (s0_ref[...] + s1_ref[...]) + (s2_ref[...] + s3_ref[...])
    mean = sums[0:8] / total_chans
    var = sums[8:16] / total_chans - mean * mean
    scale = lax.rsqrt(var + 1e-05)
    chans = gain_ref.shape[1]
    pick = iota((LANES, chans), 0) // 2 == iota((LANES, chans), 1)
    gain = jnp.sum(jnp.where(pick, gain_ref[...], 0.0), axis=1, keepdims=True)
    bias = jnp.sum(jnp.where(pick, bias_ref[...], 0.0), axis=1, keepdims=True)
    gate = silu(gate_ref[...].astype(F32))
    comb = comb_ref[...]
    means = jnp.concatenate([mean] * (LANES // 8), axis=0)
    scales = jnp.concatenate([scale] * (LANES // 8), axis=0)
    normed = (comb - means) * scales * gain + bias
    out_ref[...] = (normed * gate).astype(BF16)


VMEM = pl.BlockSpec(memory_space=pltpu.VMEM)


def call(kernel, name, outs, scratch, inputs):
    single = not isinstance(outs, (list, tuple))
    return pl.pallas_call(
        kernel,
        out_shape=outs,
        in_specs=[VMEM] * len(inputs),
        out_specs=VMEM if single else [VMEM] * len(outs),
        scratch_shapes=scratch,
        name=name,
        compiler_params=pltpu.CompilerParams(vmem_limit_bytes=24 << 20),
    )(*inputs)


def others(value):
    return [
        lax.ppermute(value, "ch", [(i, i ^ k) for i in range(lax.axis_size("ch"))])
        for k in (1, 2, 3)
    ]


def exchange(value):
    return lax.all_to_all(value, ("sp", "ch"), split_axis=0, concat_axis=0, tiled=True)


def on_device(
    x_in,
    gate_in,
    conv_weight,
    conv_bias,
    proj_weight,
    dt_weight,
    dt_bias,
    decay_rate,
    skip_gain,
    norm_gain,
    norm_bias,
):
    chans, rows, cols = x_in.shape
    total_chans = chans * lax.axis_size("ch")
    flat = (chans * rows, cols)
    struct = jax.ShapeDtypeStruct
    buffer = struct((4 * cols, LANES), BF16)

    def vm(*shape):
        return pltpu.VMEM(shape, F32)

    send, weights = call(
        prep_kernel,
        "prep",
        [buffer, struct((WBUF_ROWS, LANES), BF16)],
        [vm(4 * cols + 16, LANES), vm(VEC_ROWS, LANES)],
        [
            x_in.reshape(flat),
            conv_weight,
            conv_bias.reshape(1, chans),
            proj_weight,
            dt_weight,
            dt_bias,
            decay_rate,
            skip_gain,
        ],
    )
    shared = others(weights)
    received = exchange(send)
    send = call(
        column_kernel,
        "columns",
        buffer,
        [vm(4 * cols + 32, LANES), pltpu.VMEM((4, WBUF_ROWS, LANES), BF16)] + [vm(64, 256)] * 6,
        [received, weights] + shared,
    )
    received = exchange(send)
    combined, sums = call(
        row_kernel,
        "rows",
        [struct((LANES, cols), F32), struct((16, cols), F32)],
        [vm(4 * cols, LANES)] + [vm(cols, LANES)] * 6,
        [received, dt_weight, dt_bias, decay_rate, skip_gain],
    )
    out = call(
        lambda *refs: norm_kernel(total_chans, *refs),
        "norm",
        struct(flat, BF16),
        [],
        [combined, sums]
        + others(sums)
        + [gate_in.reshape(flat), norm_gain.reshape(1, chans), norm_bias.reshape(1, chans)],
    )
    return out.reshape(chans, rows, cols)


def solution(mesh):
    placed = (
        P("ch", "sp", None),
        P("ch", "sp", None),
        P("ch", None),
        P("ch"),
        P(None, None, "ch"),
        P(None, "ch", None),
        P(None, "ch"),
        P(None, "ch", None),
        P(None, "ch"),
        P("ch"),
        P("ch"),
    )
    return jax.shard_map(
        on_device, mesh=mesh, in_specs=placed, out_specs=P("ch", "sp", None), check_vma=False
    )
```

profile of v0, /device:TPU:1, one launch (start us, length us, event | category | flops | bytes accessed | tf_op | source)
XLA Modules:
  0.0 50.2 jit_solution(14004448314674574611)
XLA Ops:
  0.0 0.0 copy-start.9
  0.0 0.8 %copy.12.cw_ref = f32[64,9]{1,0:T(8,128)S(1)} copy(f32[64,9]{0,1:T(8,128)} %param.13) | data formatting | bytes 4608 | tf_op args[2]
  0.8 0.0 copy-done.9
  0.8 0.0 copy-start.8
  0.8 0.1 copy.13.dtw_ref
  0.9 0.7 %copy-done.8 = f32[4,64,16]{1,2,0:T(8,128)S(1)} copy-done((f32[4,64,16]{1,2,0:T(8,128)S(1)}, f32[4,64,16]{1,2,0:T(8,128)}, u32[]{:S(2)}) %copy-start.8) | copy-done | bytes 16408
  1.6 0.0 copy-start
  1.6 0.0 copy-start.1
  1.6 0.0 copy-start.4
  1.6 0.1 copy.14.rate_ref
  1.7 0.0 copy-start.3
  1.7 0.0 copy-start.5
  1.7 0.7 %copy-done = bf16[4,40,64]{2,1,0:T(8,128)(2,1)S(1)} copy-done((bf16[4,40,64]{2,1,0:T(8,128)(2,1)S(1)}, bf16[4,40,64]{2,1,0:T(8,128)(2,1)}, u32[]{:S(2)}) %copy-start) | copy-done | bytes 20504
  2.3 0.0 copy-done.1
  2.3 0.0 copy-done.4
  2.3 0.0 copy-done.3
  2.4 0.0 copy-done.5
  2.4 1.0 %prep.1 = (bf16[512,128]{1,0:T(8,128)(2,1)}, bf16[288,128]{1,0:T(8,128)(2,1)S(1)}) custom-call(bf16[128,128]{1,0:T(8,128)(2,1)S(1)} %bitcast.13, f32[64,9]{1,0:T(8,128)S(1)} %copy.12.cw_ref, f32[1,64]{1,0:T(1,128)S(1)} %bitcast.15, bf16[4,40,64]{2,1,0:T(8,128)(2,1)S(1)} %copy-done, f32[4,64,8]{2,1,0:T(8,128)S(1)} %copy.13.dtw_ref, f32[4,64]{1,0:T(4,128)S(1)} %copy-done.3, ...), custom_call_target="tpu_custom_call" | custom-call | tf_op jit(solution)/shard_map/prep/pallas_call | solution.py:297
  3.4 11.5 %all-to-all-start = ((bf16[128,4,128]{2,1,0:T(4,128)(2,1)}), bf16[128,4,128]{2,1,0:T(4,128)(2,1)S(1)}, u32[]{:S(2)}, u32[]{:S(2)}) async-start(bf16[128,4,128]{2,1,0:T(4,128)(2,1)} %bitcast.2), calls=%async_computation | async-start | bytes 262144 | tf_op jit(solution)/shard_map/all_to_all | solution.py:316
  14.9 1.8 %collective-permute-start.2 = (bf16[288,128]{1,0:T(8,128)(2,1)S(1)}, bf16[288,128]{1,0:T(8,128)(2,1)S(1)}, u32[]{:S(2)}, u32[]{:S(2)}) collective-permute-start(bf16[288,128]{1,0:T(8,128)(2,1)S(1)} %get-tuple-element.10.own_ref), channel_id=1, source_target_pairs={{0,3},{1,2},{2,1},{3,0},{4,7},{5,6},{6,5},{7,4},{8,11},{9,10},{10,... | collective-permute-start | bytes 221192 | tf_op jit(solution)/shard_map/ppermute | solution.py:310
  16.7 0.7 %collective-permute-start.1 = (bf16[288,128]{1,0:T(8,128)(2,1)S(1)}, bf16[288,128]{1,0:T(8,128)(2,1)S(1)}, u32[]{:S(2)}, u32[]{:S(2)}) collective-permute-start(bf16[288,128]{1,0:T(8,128)(2,1)S(1)} %get-tuple-element.10.own_ref), channel_id=1, source_target_pairs={{0,2},{1,3},{2,0},{3,1},{4,6},{5,7},{6,4},{7,5},{8,10},{9,11},{10,... | collective-permute-start | bytes 221192 | tf_op jit(solution)/shard_map/ppermute | solution.py:310
  17.4 0.0 collective-permute-start
  17.4 2.6 %collective-permute-done.2.w3_ref = bf16[288,128]{1,0:T(8,128)(2,1)S(1)} collective-permute-done((bf16[288,128]{1,0:T(8,128)(2,1)S(1)}, bf16[288,128]{1,0:T(8,128)(2,1)S(1)}, u32[]{:S(2)}, u32[]{:S(2)}) %collective-permute-start.2) | collective-permute-done | bytes 73760 | tf_op jit(solution)/shard_map/ppermute | solution.py:310
  19.9 2.7 %collective-permute-done.1.w2_ref = bf16[288,128]{1,0:T(8,128)(2,1)S(1)} collective-permute-done((bf16[288,128]{1,0:T(8,128)(2,1)S(1)}, bf16[288,128]{1,0:T(8,128)(2,1)S(1)}, u32[]{:S(2)}, u32[]{:S(2)}) %collective-permute-start.1) | collective-permute-done | bytes 73760 | tf_op jit(solution)/shard_map/ppermute | solution.py:310
  22.6 0.0 collective-permute-done.w1_ref
  22.6 2.4 %all-to-all-done = bf16[128,4,128]{2,1,0:T(4,128)(2,1)S(1)} async-done(((bf16[128,4,128]{2,1,0:T(4,128)(2,1)}), bf16[128,4,128]{2,1,0:T(4,128)(2,1)S(1)}, u32[]{:S(2)}, u32[]{:S(2)}) %all-to-all-start) | async-done | bytes 131104 | tf_op jit(solution)/shard_map/all_to_all | solution.py:316
  25.0 1.9 %columns.1 = bf16[512,128]{1,0:T(8,128)(2,1)S(1)} custom-call(bf16[512,128]{1,0:T(8,128)(2,1)S(1)} %bitcast.10, bf16[288,128]{1,0:T(8,128)(2,1)S(1)} %get-tuple-element.10.own_ref, bf16[288,128]{1,0:T(8,128)(2,1)S(1)} %collective-permute-done.w1_ref, bf16[288,128]{1,0:T(8,128)(2,1)S(1)} %collective-permute-done.1.w2_ref, ...), custom_call_target="tpu_custom_call" | custom-call | tf_op jit(solution)/shard_map/columns/pallas_call | solution.py:297
  27.0 16.4 %all_to_all.22 = bf16[128,4,128]{2,1,0:T(4,128)(2,1)S(1)} all-to-all(bf16[128,4,128]{2,1,0:T(4,128)(2,1)S(1)} %bitcast.11), channel_id=1, replica_groups=mesh['sp'=32,'ch'=4] {'sp','ch'}, dimensions={0} | all-to-all | bytes 262144 | tf_op jit(solution)/shard_map/all_to_all | solution.py:316
  43.3 0.0 copy-start.2
  43.3 2.0 %rows.1 = (f32[128,128]{1,0:T(8,128)S(1)}, f32[16,128]{1,0:T(8,128)S(1)}) custom-call(bf16[512,128]{1,0:T(8,128)(2,1)S(1)} %bitcast.12, f32[4,64,8]{2,1,0:T(8,128)S(1)} %copy.13.dtw_ref, f32[4,64]{1,0:T(4,128)S(1)} %copy-done.3, f32[4,64,16]{2,1,0:T(8,128)S(1)} %copy.14.rate_ref, f32[4,64]{1,0:T(4,128)S(1)} %copy-done.4), custom_call_target="tpu_custom_call" | custom-call | tf_op jit(solution)/shard_map/rows/pallas_call | solution.py:297
  45.4 0.9 %collective-permute-start.5 = (f32[16,128]{1,0:T(8,128)S(1)}, f32[16,128]{1,0:T(8,128)S(1)}, u32[]{:S(2)}, u32[]{:S(2)}) collective-permute-start(f32[16,128]{1,0:T(8,128)S(1)} %get-tuple-element.12.refs_1_), channel_id=1, source_target_pairs={{0,3},{1,2},{2,1},{3,0},{4,7},{5,6},{6,5},{7,4},{8,11},{9,10},{10,... | collective-permute-start | bytes 24584 | tf_op jit(solution)/shard_map/ppermute | solution.py:310
  46.3 0.9 %collective-permute-start.4 = (f32[16,128]{1,0:T(8,128)S(1)}, f32[16,128]{1,0:T(8,128)S(1)}, u32[]{:S(2)}, u32[]{:S(2)}) collective-permute-start(f32[16,128]{1,0:T(8,128)S(1)} %get-tuple-element.12.refs_1_), channel_id=1, source_target_pairs={{0,2},{1,3},{2,0},{3,1},{4,6},{5,7},{6,4},{7,5},{8,10},{9,11},{10,... | collective-permute-start | bytes 24584 | tf_op jit(solution)/shard_map/ppermute | solution.py:310
  47.2 0.4 collective-permute-start.3
  47.6 0.9 %collective-permute-done.5.refs_4_ = f32[16,128]{1,0:T(8,128)S(1)} collective-permute-done((f32[16,128]{1,0:T(8,128)S(1)}, f32[16,128]{1,0:T(8,128)S(1)}, u32[]{:S(2)}, u32[]{:S(2)}) %collective-permute-start.5) | collective-permute-done | bytes 8224 | tf_op jit(solution)/shard_map/ppermute | solution.py:310
  48.5 0.3 collective-permute-done.4.refs_3_
  48.8 0.0 collective-permute-done.3.refs_2_
  48.8 0.0 copy-start.6
  48.8 0.0 copy-start.7
  48.8 0.0 copy-done.2
  48.8 0.6 %copy-done.6 = f32[64]{0:T(128)S(1)} copy-done((f32[64]{0:T(128)S(1)}, f32[64]{0:T(128)}, u32[]{:S(2)}) %copy-start.6) | copy-done | bytes 280
  49.4 0.0 copy-done.7
  49.5 0.7 %norm.1 = bf16[128,128]{1,0:T(8,128)(2,1)} custom-call(f32[128,128]{1,0:T(8,128)S(1)} %get-tuple-element.11.refs_0_, f32[16,128]{1,0:T(8,128)S(1)} %get-tuple-element.12.refs_1_, f32[16,128]{1,0:T(8,128)S(1)} %collective-permute-done.3.refs_2_, f32[16,128]{1,0:T(8,128)S(1)} %collective-permute-done.4.refs_3_, f32[16,128]{1,0:T(8,128)S(1)} %collective-permute-done.5.refs_4_, ...), custom_call_target="tpu_custom_call" | custom-call | tf_op jit(solution)/shard_map/norm/pallas_call | solution.py:297
Async XLA Ops:
  0.0 0.8 %copy-start.9 = (f32[4,64,8]{1,2,0:T(8,128)S(1)}, f32[4,64,8]{1,2,0:T(8,128)}, u32[]{:S(2)}) copy-start(f32[4,64,8]{1,2,0:T(8,128)} %param.16) | copy-start | bytes 24580
  0.8 0.8 %copy-start.8 = (f32[4,64,16]{1,2,0:T(8,128)S(1)}, f32[4,64,16]{1,2,0:T(8,128)}, u32[]{:S(2)}) copy-start(f32[4,64,16]{1,2,0:T(8,128)} %param.18) | copy-start | bytes 49156
  1.6 0.8 %copy-start = (bf16[4,40,64]{2,1,0:T(8,128)(2,1)S(1)}, bf16[4,40,64]{2,1,0:T(8,128)(2,1)}, u32[]{:S(2)}) copy-start(bf16[4,40,64]{2,1,0:T(8,128)(2,1)} %pw_ref.1) | copy-start | bytes 61444
  1.6 0.8 %copy-start.1 = (bf16[64,2,128]{2,1,0:T(2,128)(2,1)S(1)}, bf16[64,2,128]{2,1,0:T(2,128)(2,1)}, u32[]{:S(2)}) copy-start(bf16[64,2,128]{2,1,0:T(2,128)(2,1)} %param.11) | copy-start | bytes 98308
  1.6 0.8 %copy-start.4 = (f32[4,64]{1,0:T(4,128)S(1)}, f32[4,64]{1,0:T(4,128)}, u32[]{:S(2)}) copy-start(f32[4,64]{1,0:T(4,128)} %skip_ref.3) | copy-start | bytes 3076
  1.7 0.7 %copy-start.3 = (f32[4,64]{1,0:T(4,128)S(1)}, f32[4,64]{1,0:T(4,128)}, u32[]{:S(2)}) copy-start(f32[4,64]{1,0:T(4,128)} %dtb_ref.3) | copy-start | bytes 3076
  1.7 0.7 %copy-start.5 = (f32[64]{0:T(128)S(1)}, f32[64]{0:T(128)}, u32[]{:S(2)}) copy-start(f32[64]{0:T(128)} %param.14) | copy-start | bytes 772
  3.4 21.7 %all-to-all-start = ((bf16[128,4,128]{2,1,0:T(4,128)(2,1)}), bf16[128,4,128]{2,1,0:T(4,128)(2,1)S(1)}, u32[]{:S(2)}, u32[]{:S(2)}) async-start(bf16[128,4,128]{2,1,0:T(4,128)(2,1)} %bitcast.2), calls=%async_computation | async-start | bytes 262144 | tf_op jit(solution)/shard_map/all_to_all | solution.py:316
  14.9 5.1 %collective-permute-start.2 = (bf16[288,128]{1,0:T(8,128)(2,1)S(1)}, bf16[288,128]{1,0:T(8,128)(2,1)S(1)}, u32[]{:S(2)}, u32[]{:S(2)}) collective-permute-start(bf16[288,128]{1,0:T(8,128)(2,1)S(1)} %get-tuple-element.10.own_ref), channel_id=1, source_target_pairs={{0,3},{1,2},{2,1},{3,0},{4,7},{5,6},{6,5},{7,4},{8,11},{9,10},{10,... | collective-permute-start | bytes 221192 | tf_op jit(solution)/shard_map/ppermute | solution.py:310
  16.7 5.9 %collective-permute-start.1 = (bf16[288,128]{1,0:T(8,128)(2,1)S(1)}, bf16[288,128]{1,0:T(8,128)(2,1)S(1)}, u32[]{:S(2)}, u32[]{:S(2)}) collective-permute-start(bf16[288,128]{1,0:T(8,128)(2,1)S(1)} %get-tuple-element.10.own_ref), channel_id=1, source_target_pairs={{0,2},{1,3},{2,0},{3,1},{4,6},{5,7},{6,4},{7,5},{8,10},{9,11},{10,... | collective-permute-start | bytes 221192 | tf_op jit(solution)/shard_map/ppermute | solution.py:310
  17.4 5.3 %collective-permute-start = (bf16[288,128]{1,0:T(8,128)(2,1)S(1)}, bf16[288,128]{1,0:T(8,128)(2,1)S(1)}, u32[]{:S(2)}, u32[]{:S(2)}) collective-permute-start(bf16[288,128]{1,0:T(8,128)(2,1)S(1)} %get-tuple-element.10.own_ref), channel_id=1, source_target_pairs={{0,1},{1,0},{2,3},{3,2},{4,5},{5,4},{6,7},{7,6},{8,9},{9,8},{10,11... | collective-permute-start | bytes 221192 | tf_op jit(solution)/shard_map/ppermute | solution.py:310
  43.3 5.5 %copy-start.2 = (bf16[64,2,128]{2,1,0:T(2,128)(2,1)S(1)}, bf16[64,2,128]{2,1,0:T(2,128)(2,1)}, u32[]{:S(2)}) copy-start(bf16[64,2,128]{2,1,0:T(2,128)(2,1)} %param.12) | copy-start | bytes 98308
  45.4 3.2 %collective-permute-start.5 = (f32[16,128]{1,0:T(8,128)S(1)}, f32[16,128]{1,0:T(8,128)S(1)}, u32[]{:S(2)}, u32[]{:S(2)}) collective-permute-start(f32[16,128]{1,0:T(8,128)S(1)} %get-tuple-element.12.refs_1_), channel_id=1, source_target_pairs={{0,3},{1,2},{2,1},{3,0},{4,7},{5,6},{6,5},{7,4},{8,11},{9,10},{10,... | collective-permute-start | bytes 24584 | tf_op jit(solution)/shard_map/ppermute | solution.py:310
  46.3 2.5 %collective-permute-start.4 = (f32[16,128]{1,0:T(8,128)S(1)}, f32[16,128]{1,0:T(8,128)S(1)}, u32[]{:S(2)}, u32[]{:S(2)}) collective-permute-start(f32[16,128]{1,0:T(8,128)S(1)} %get-tuple-element.12.refs_1_), channel_id=1, source_target_pairs={{0,2},{1,3},{2,0},{3,1},{4,6},{5,7},{6,4},{7,5},{8,10},{9,11},{10,... | collective-permute-start | bytes 24584 | tf_op jit(solution)/shard_map/ppermute | solution.py:310
  47.2 1.6 %collective-permute-start.3 = (f32[16,128]{1,0:T(8,128)S(1)}, f32[16,128]{1,0:T(8,128)S(1)}, u32[]{:S(2)}, u32[]{:S(2)}) collective-permute-start(f32[16,128]{1,0:T(8,128)S(1)} %get-tuple-element.12.refs_1_), channel_id=1, source_target_pairs={{0,1},{1,0},{2,3},{3,2},{4,5},{5,4},{6,7},{7,6},{8,9},{9,8},{10,11... | collective-permute-start | bytes 24584 | tf_op jit(solution)/shard_map/ppermute | solution.py:310
  48.8 0.7 %copy-start.6 = (f32[64]{0:T(128)S(1)}, f32[64]{0:T(128)}, u32[]{:S(2)}) copy-start(f32[64]{0:T(128)} %param.20) | copy-start | bytes 772
  48.8 0.7 %copy-start.7 = (f32[64]{0:T(128)S(1)}, f32[64]{0:T(128)}, u32[]{:S(2)}) copy-start(f32[64]{0:T(128)} %param.21) | copy-start | bytes 772
where the time goes:
time: 50.5 us; the launch traced here: 50.2 us
  blocking collectives  16.4 us (32%)
  starting transfers between devices  16.2 us (32%)
  waiting for transfers between devices  8.88 us (18%)
  Pallas kernels  5.67 us (11%)
  local copies, waits for them, and re-layouts  2.98 us (6%)
    all_to_all x1, blocking collectives, exchange(): lax.all_to_all(value, ('sp', 'ch'), split_axis=0, concat_axis=0, tiled=True)  16.4 us
    all_to_all x1, starting transfers between devices, exchange(): lax.all_to_all(value, ('sp', 'ch'), split_axis=0, concat_axis=0, tiled=True)  11.5 us
    ppermute x6, waiting for transfers between devices, others(): lax.ppermute(value, 'ch', [(i, i ^ k) for i in range(lax.axis_size('ch'))])  6.45 us
    pallas_call x4, Pallas kernels, call(): pl.pallas_call(kernel, out_shape=outs, in_specs=[VMEM] * len(inputs), out...  5.67 us
    ppermute x6, starting transfers between devices, others(): lax.ppermute(value, 'ch', [(i, i ^ k) for i in range(lax.axis_size('ch'))])  4.72 us
    unnamed x23, local copies, waits for them, and re-layouts  2.98 us
    all_to_all x1, waiting for transfers between devices, exchange(): lax.all_to_all(value, ('sp', 'ch'), split_axis=0, concat_axis=0, tiled=True)  2.42 us
  transfers between devices with their start and end apart: 7, of which 5 were waited for; matrix products, arithmetic and copies ran while one was open for 0% of the time, Pallas kernels for 0%

commit v1 on v0

v1 whole, which is shorter than its diff:
```python
import math

import jax
import jax.numpy as jnp
from jax import lax
from jax.experimental import pallas as pl
from jax.experimental.pallas import tpu as pltpu
from jax.sharding import PartitionSpec as P

F32 = jnp.float32
BF16 = jnp.bfloat16
LANES = 128
EXACT = lax.Precision.HIGHEST
NEG_LOG2E = -1.0 / math.log(2.0)

CHUNK = 8
X_ROWS = 3
PROJ_PAIRS = 80
VEC_PAIRS = 32


def iota(shape, axis):
    return lax.broadcasted_iota(jnp.int32, shape, axis)


def spread(chans, offset):
    lane = iota((chans, 2 * chans), 1)
    return jnp.where(lane == 2 * iota((chans, 2 * chans), 0) + offset, 1.0, 0.0).astype(F32)


def dup_rows(value, dup):
    return jnp.dot(value, dup, preferred_element_type=F32, precision=EXACT)


def softplus(x):
    return jnp.maximum(x, 0.0) + jnp.log1p(jnp.exp(-jnp.abs(x)))


def silu(x):
    return x * jax.nn.sigmoid(x)


def roll(x, shift, axis):
    return pltpu.roll(x, shift % x.shape[axis], axis)


def prep_kernel(*refs):
    count = 8
    sources, send_ref, scr, vec, packed = refs[:count], *refs[count : count + 4]
    loaded, arrived = refs[count + 4 : -1], refs[-1]
    copies = [
        pltpu.make_async_copy(source, target, arrived.at[index])
        for index, (source, target) in enumerate(zip(sources, loaded))
    ]
    for copy in copies:
        copy.start()
    for copy in copies:
        copy.wait()
    x_ref, cw_ref, cb_ref, pw_ref, dtw_ref, dtb_ref, rate_ref, skip_ref = loaded
    chans = cw_ref.shape[1]
    even, odd = spread(chans, 0), spread(chans, 1)
    even_b, odd_b = even.astype(BF16), odd.astype(BF16)
    half = VEC_PAIRS
    vec[0:9, :] = cw_ref[...]
    vec[9:10, :] = cb_ref[...]
    vec[10:12, :] = dtb_ref[2:4, :]
    vec[12:14, :] = skip_ref[2:4, :]
    vec[14:16, :] = jnp.zeros((2, chans), F32)
    vec[16:24, :] = dtw_ref[2]
    vec[24:32, :] = dtw_ref[3]
    vec[32:48, :] = rate_ref[2]
    vec[48:64, :] = rate_ref[3]
    whole = vec[...]
    high = whole.astype(BF16)
    low = (whole - high.astype(F32)).astype(BF16)

    def pack(first, second):
        return jnp.dot(first, even_b, preferred_element_type=F32) + jnp.dot(
            second, odd_b, preferred_element_type=F32
        )

    third = pw_ref[2].astype(F32)
    fourth = pw_ref[3].astype(F32)
    rest = jnp.concatenate([third[0:8], fourth[0:8], third[8:40], fourth[8:40]], axis=0)
    packed[0:40, :] = pack(pw_ref[0], rest[0:40].astype(BF16))
    packed[40:80, :] = pack(pw_ref[1], rest[40:80].astype(BF16))
    packed[80:112, :] = pack(high[0:half], high[half:])
    packed[112:144, :] = pack(low[0:half], low[half:])
    packed[144:160, :] = jnp.zeros((16, LANES), F32)

    turned = x_ref[...].astype(F32).T
    base = 2 * CHUNK
    scr[pl.ds(base + CHUNK, LANES, stride=CHUNK), :] = turned
    scr[pl.ds(base + 1, LANES, stride=CHUNK), :] = turned
    scr[pl.ds(base - CHUNK + 2, LANES, stride=CHUNK), :] = turned
    scr[base : base + 1, :] = jnp.zeros((1, LANES), F32)
    last = base + CHUNK * (LANES - 1) + 2
    scr[last : last + 1, :] = jnp.zeros((1, LANES), F32)
    slab = lax.axis_index("sp")
    for piece in range(CHUNK - X_ROWS):
        row = packed[pl.ds(32 * piece + slab, 1), :]
        scr[pl.ds(base + X_ROWS + piece, LANES, stride=CHUNK), :] = jnp.broadcast_to(row, (LANES, LANES))
    send_ref[...] = scr[base : base + CHUNK * LANES, :].astype(BF16)


def scan_pair(steps, rates, delta_ref, drive_ref, b_at, c_at, part_ref, row_of):
    blocks = delta_ref.shape[1]
    shape = (16, LANES)
    states = [[jnp.zeros(shape, F32) for _ in range(blocks)] for _ in range(2)]
    for step in range(steps):
        for way in range(2):
            at = step if way == 0 else steps - 1 - step
            row = row_of(at)
            b_now, c_now = b_at(way, at), c_at(way, at)
            for block in range(blocks):
                delta = delta_ref[way, block, row : row + 1, :]
                drive = drive_ref[way, block, row : row + 1, :]
                decay = jnp.exp2(delta * rates[way][block])
                state = decay * states[way][block] + drive * b_now
                states[way][block] = state
                product = c_now * state
                part_ref[way, block, 8 * row : 8 * row + 8, :] = product[0:8] + product[8:16]


def outputs_of(part_ref, block, half_ref):
    rows = part_ref.shape[2] // 8
    total = None
    for way in range(2):
        for lane_row in range(4):
            term = part_ref[way, block, pl.ds(lane_row, 2 * rows, stride=4), :]
            total = term if total is None else total + term
    half_ref[0 : 2 * rows, :] = total
    return half_ref[pl.ds(0, rows, stride=2), :] + half_ref[pl.ds(1, rows, stride=2), :]


def halves(value):
    high = value.astype(BF16)
    return high, (value - high.astype(F32)).astype(BF16)


def two_part_dot(value, high, low):
    return jnp.dot(value, high, preferred_element_type=F32) + jnp.dot(
        value, low, preferred_element_type=F32
    )


def column_kernel(recv_ref, send_ref, flat_scr, scr, delta_scr, drive_scr, part_scr, half_scr, turned_scr):
    slabs = LANES // 4
    pad = 8
    flat_scr[...] = recv_ref[...].astype(F32)
    for row in range(CHUNK):
        scr[row, pad - 4 : pad, :] = jnp.zeros((4, LANES), F32)
        scr[row, pad + LANES : pad + LANES + 4, :] = jnp.zeros((4, LANES), F32)
        scr[row, pad : pad + LANES, :] = flat_scr[pl.ds(row, LANES, stride=CHUNK), :]

    even = iota((slabs, LANES), 1) % 2 == 0
    vecs = []
    projs = []
    conv = []
    for group in range(4):

        def rows_of(row, shift):
            return scr[row, pl.ds(pad + group + 4 * shift, slabs, stride=4), :]

        pieces = [rows_of(row, 0) for row in range(X_ROWS, CHUNK)]
        projs.append([pieces[0], pieces[1], pieces[2][0:16]])
        vec = jnp.concatenate([pieces[2][16:32], pieces[3][0:16]], axis=0) + jnp.concatenate(
            [pieces[3][16:32], pieces[4][0:16]], axis=0
        )
        vecs.append(vec)
        taps = jnp.where(even[0:16], vec[0:16], roll(vec[0:16], 1, 1))
        total = jnp.zeros((slabs, LANES), F32) + taps[9:10, :]
        for side in range(3):
            here = rows_of(side, 0)
            up = jnp.where(even, roll(rows_of(side, -1), -1, 1), roll(here, 1, 1))
            down = jnp.where(even, roll(here, -1, 1), roll(rows_of(side, 1), 1, 1))
            total = total + taps[side : side + 1, :] * up
            total = total + taps[3 + side : 4 + side, :] * here
            total = total + taps[6 + side : 7 + side, :] * down
        conv.append(silu(total).astype(BF16).astype(F32))

    def from_even(left, right):
        mask = iota(left.shape, 1) % 2 == 0
        return jnp.where(mask, left, roll(right, 1, 1))

    def from_odd(left, right):
        mask = iota(left.shape, 1) % 2 == 0
        return jnp.where(mask, roll(left, -1, 1), right)

    def all_groups(take, parts):
        return jnp.concatenate([take(parts[0], parts[1]), take(parts[2], parts[3])], axis=1)

    values = jnp.concatenate([all_groups(from_even, conv), all_groups(from_odd, conv)], axis=0)
    values_b = values.astype(BF16)
    proj_w = jnp.concatenate(
        [
            all_groups(take, [p[piece] for p in projs])
            for take in (from_even, from_odd)
            for piece in range(3)
        ],
        axis=0,
    ).astype(BF16)
    vec = jnp.concatenate([all_groups(from_even, vecs), all_groups(from_odd, vecs)], axis=0)

    nt = (((1,), (1,)), ((), ()))
    proj = lax.dot_general(values_b, proj_w[0:128], nt, preferred_element_type=F32)
    proj = proj.astype(BF16).astype(F32)
    turned = lax.dot_general(proj_w[96:160], values_b, nt, preferred_element_type=F32)
    turned = turned.astype(BF16).astype(F32)

    turned_scr[...] = turned
    low = lax.dot_general(values_b, proj_w[80:96], nt, preferred_element_type=F32).astype(BF16)
    dt_rows = vec[16:32]
    second_half = iota((16, 256), 0) >= 8
    rates = []
    for way in range(2):
        chosen = jnp.where(second_half == (way == 1), dt_rows, 0.0)
        delta = softplus(two_part_dot(low, *halves(chosen)) + vec[10 + way : 11 + way, :])
        drive = delta * values
        scaled = vec[32 + 16 * way : 48 + 16 * way] * NEG_LOG2E
        rates.append([scaled[:, 0:LANES], scaled[:, LANES:]])
        for block in range(2):
            lanes = slice(LANES * block, LANES * block + LANES)
            delta_scr[way, block] = delta[:, lanes]
            drive_scr[way, block] = drive[:, lanes]

    def row_of(at):
        return (at % 2) * slabs + at // 2

    def part(way, at, offset):
        column = row_of(at)
        first = 32 * way + offset
        return jnp.broadcast_to(turned_scr[first : first + 16, column : column + 1], (16, LANES))

    scan_pair(
        2 * slabs,
        rates,
        delta_scr,
        drive_scr,
        lambda way, at: part(way, at, 0),
        lambda way, at: part(way, at, 16),
        part_scr,
        row_of,
    )

    skip = vec[12:13] + vec[13:14]
    for block in range(2):
        lanes = slice(LANES * block, LANES * block + LANES)
        y = outputs_of(part_scr, block, half_scr) + skip[:, lanes] * values[:, lanes]
        y_even, y_odd = y[0:slabs], y[slabs:]
        backs = (
            jnp.where(even, y_even, roll(y_odd, 1, 1)),
            jnp.where(even, roll(y_even, -1, 1), y_odd),
        )
        for bit in range(2):
            group = 2 * block + bit
            parts = (backs[bit], conv[group], proj[0:slabs], proj[slabs:])
            for row in range(4):
                scr[row, pl.ds(group, slabs, stride=4), :] = parts[row]
    for row in range(4):
        flat_scr[pl.ds(row, LANES, stride=4), :] = scr[row, 0:LANES, :]
    send_ref[...] = flat_scr[0 : 4 * LANES, :].astype(BF16)


def side_kernel(
    dtw_ref,
    dtb_ref,
    rate_ref,
    skip_ref,
    gain_ref,
    bias_ref,
    gate_ref,
    vec_ref,
    high_ref,
    low_ref,
    gate_out_ref,
    affine_ref,
):
    chans = dtw_ref.shape[2]
    dup = spread(chans, 0) + spread(chans, 1)
    vec_ref[0:16, :] = dup_rows(rate_ref[0], dup) * NEG_LOG2E
    vec_ref[16:32, :] = dup_rows(rate_ref[1], dup) * NEG_LOG2E
    vec_ref[32:36, :] = dup_rows(dtb_ref[...], dup)
    skip = dup_rows(skip_ref[...], dup)
    vec_ref[36:37, :] = skip[0:1] + skip[1:2]
    vec_ref[37:40, :] = jnp.zeros((3, LANES), F32)
    lane_row = iota((8, LANES), 1) % 2
    columns = []
    for way in range(2):
        dt_rows = dup_rows(dtw_ref[way], dup)
        column = []
        for row in range(2):
            column += [jnp.zeros((40 * way, LANES), F32)] if way else []
            column.append(jnp.where(lane_row == row, dt_rows, 0.0))
            column.append(jnp.zeros((LANES - 40 * way - 8, LANES), F32))
        columns.append(jnp.concatenate(column, axis=0))
    high_ref[...], low_ref[...] = halves(jnp.concatenate(columns, axis=1))
    gate_out_ref[...] = silu(gate_ref[...].astype(F32))
    pick = iota((LANES, LANES), 0) == iota((LANES, LANES), 1)
    for index, ref in enumerate((gain_ref, bias_ref)):
        lanes = dup_rows(ref[...], dup)
        column = jnp.sum(jnp.where(pick, lanes, 0.0), axis=1, keepdims=True)
        affine_ref[index] = jnp.broadcast_to(column, (LANES, LANES))


def row_kernel(
    recv_ref,
    vec_ref,
    high_ref,
    low_ref,
    comb_ref,
    sums_ref,
    scr,
    mixed_scr,
    delta_scr,
    drive_scr,
    part_scr,
    half_scr,
    turned_scr,
):
    cols = LANES
    scr[...] = recv_ref[...].astype(F32)
    vertical = scr[pl.ds(0, cols, stride=4), :]
    values = scr[pl.ds(1, cols, stride=4), :]
    proj = [scr[pl.ds(2 + row, cols, stride=4), :] for row in range(2)]

    both = jnp.concatenate(proj, axis=1).astype(BF16)
    low_rank = two_part_dot(both, high_ref[...], low_ref[...])
    rates = []
    for way in range(2):
        lanes = slice(LANES * way, LANES * way + LANES)
        delta = softplus(low_rank[:, lanes] + vec_ref[32 + way : 33 + way, :])
        delta_scr[way, 0] = delta
        drive_scr[way, 0] = delta * values
        rates.append([vec_ref[16 * way : 16 * way + 16, :]])

    for row in range(2):
        mixed_scr[pl.ds(row, cols, stride=2), :] = proj[row]
    turned_scr[...] = mixed_scr[...].T
    parity = iota((16, LANES), 1) % 2

    def part(way, at, offset):
        first = 40 * way + offset
        start = LANES * (at // 64)
        return jnp.take_along_axis(
            turned_scr[first : first + 16, start : start + LANES],
            parity + 2 * (at % 64),
            axis=1,
            mode="promise_in_bounds",
        )

    scan_pair(
        cols,
        rates,
        delta_scr,
        drive_scr,
        lambda way, at: part(way, at, 8),
        lambda way, at: part(way, at, 24),
        part_scr,
        lambda at: at,
    )
    combined = outputs_of(part_scr, 0, half_scr) + vec_ref[36:37, :] * values + vertical
    turned_back = combined.T
    comb_ref[...] = turned_back
    for index, value in enumerate((turned_back, turned_back * turned_back)):
        part_sum = value[0:8]
        for tile in range(1, LANES // 8):
            part_sum = part_sum + value[8 * tile : 8 * tile + 8]
        part_sum = part_sum + roll(part_sum, 4, 0)
        part_sum = part_sum + roll(part_sum, 2, 0)
        sums_ref[8 * index : 8 * index + 8, :] = part_sum


def norm_kernel(total_chans, comb_ref, s0_ref, s1_ref, s2_ref, s3_ref, gate_ref, affine_ref, out_ref):
    sums = (s0_ref[...] + s1_ref[...]) + (s2_ref[...] + s3_ref[...])
    mean = sums[0:8] / total_chans
    var = sums[8:16] / total_chans - mean * mean
    scale = lax.rsqrt(var + 1e-05)
    comb = comb_ref[...]
    means = jnp.concatenate([mean] * (LANES // 8), axis=0)
    scales = jnp.concatenate([scale] * (LANES // 8), axis=0)
    normed = (comb - means) * scales * affine_ref[0] + affine_ref[1]
    out_ref[...] = (normed * gate_ref[...]).astype(BF16)


VMEM = pl.BlockSpec(memory_space=pltpu.VMEM)


def call(kernel, name, outs, scratch, inputs, place=VMEM, grant=24 << 20):
    single = not isinstance(outs, (list, tuple))
    return pl.pallas_call(
        kernel,
        out_shape=outs,
        in_specs=[place] * len(inputs),
        out_specs=VMEM if single else [VMEM] * len(outs),
        scratch_shapes=scratch,
        name=name,
        compiler_params=pltpu.CompilerParams(vmem_limit_bytes=grant),
    )(*inputs)


def others(value):
    return [
        lax.ppermute(value, "ch", [(i, i ^ k) for i in range(lax.axis_size("ch"))])
        for k in (1, 2, 3)
    ]


def exchange(value):
    return lax.all_to_all(value, ("sp", "ch"), split_axis=0, concat_axis=0, tiled=True)


def on_device(
    x_in,
    gate_in,
    conv_weight,
    conv_bias,
    proj_weight,
    dt_weight,
    dt_bias,
    decay_rate,
    skip_gain,
    norm_gain,
    norm_bias,
):
    chans, rows, cols = x_in.shape
    total_chans = chans * lax.axis_size("ch")
    flat = (chans * rows, cols)
    struct = jax.ShapeDtypeStruct

    def vm(*shape):
        return pltpu.VMEM(shape, F32)

    dt_weight = dt_weight.transpose(0, 2, 1)
    decay_rate = decay_rate.transpose(0, 2, 1)
    arguments = [
        x_in.reshape(flat),
        conv_weight.T,
        conv_bias.reshape(1, chans),
        proj_weight,
        dt_weight,
        dt_bias,
        decay_rate,
        skip_gain,
    ]
    send = call(
        prep_kernel,
        "prep",
        struct((CHUNK * cols, LANES), BF16),
        [vm(CHUNK * (cols + 4), LANES), vm(2 * VEC_PAIRS, chans), vm(160, LANES)]
        + [pltpu.VMEM(value.shape, value.dtype) for value in arguments]
        + [pltpu.SemaphoreType.DMA((len(arguments),))],
        [pltpu.with_memory_space_constraint(value, pltpu.HBM) for value in arguments],
        pl.BlockSpec(memory_space=pltpu.HBM),
    )
    vec, high, low, gate, affine = call(
        side_kernel,
        "side",
        [
            struct((40, LANES), F32),
            struct((2 * LANES, 2 * LANES), BF16),
            struct((2 * LANES, 2 * LANES), BF16),
            struct((LANES, cols), F32),
            struct((2, LANES, cols), F32),
        ],
        [],
        [
            dt_weight,
            dt_bias,
            decay_rate,
            skip_gain,
            norm_gain.reshape(1, chans),
            norm_bias.reshape(1, chans),
            gate_in.reshape(flat),
        ],
    )
    send = call(
        column_kernel,
        "columns",
        struct((4 * cols, LANES), BF16),
        [
            vm(CHUNK * cols, LANES),
            vm(CHUNK, cols + 16, LANES),
            vm(2, 2, 64, LANES),
            vm(2, 2, 64, LANES),
            vm(2, 2, 8 * 64, LANES),
            vm(LANES, LANES),
            vm(64, 64),
        ],
        [exchange(send)],
    )
    received = exchange(send)
    combined, sums = call(
        row_kernel,
        "rows",
        [struct((LANES, cols), F32), struct((16, cols), F32)],
        [
            vm(4 * cols, LANES),
            vm(2 * cols, LANES),
            vm(2, 1, cols, LANES),
            vm(2, 1, cols, LANES),
            vm(2, 1, 8 * cols, LANES),
            vm(2 * cols, LANES),
            vm(LANES, 2 * cols),
        ],
        [received, vec, high, low],
    )
    out = call(
        lambda *refs: norm_kernel(total_chans, *refs),
        "norm",
        struct(flat, BF16),
        [],
        [combined, sums] + others(sums) + [gate, affine],
    )
    return out.reshape(chans, rows, cols)


def solution(mesh):
    placed = (
        P("ch", "sp", None),
        P("ch", "sp", None),
        P("ch", None),
        P("ch"),
        P(None, None, "ch"),
        P(None, "ch", None),
        P(None, "ch"),
        P(None, "ch", None),
        P(None, "ch"),
        P("ch"),
        P("ch"),
    )
    return jax.shard_map(
        on_device, mesh=mesh, in_specs=placed, out_specs=P("ch", "sp", None), check_vma=False
    )
```

time: 50.5 us -> 46.5 us (0.921)
  starting transfers between devices: 16.2 us -> 6.12 us
  blocking collectives: 16.4 us -> 22.7 us
  local copies, waits for them, and re-layouts: 2.98 us -> 0.65 us
  waiting for transfers between devices: 8.88 us -> 10.4 us
  Pallas kernels: 5.67 us -> 6.31 us
    all_to_all x1, starting transfers between devices: 11.5 us -> 3.9 us  [exchange(): lax.all_to_all(value, ('sp', 'ch'), split_axis=0, concat_axis=0, tiled=True)]
    all_to_all x1, waiting for transfers between devices: 2.42 us -> 9.17 us  [exchange(): lax.all_to_all(value, ('sp', 'ch'), split_axis=0, concat_axis=0, tiled=True)]
    all_to_all x1, blocking collectives: 16.4 us -> 22.7 us  [exchange(): lax.all_to_all(value, ('sp', 'ch'), split_axis=0, concat_axis=0, tiled=True)]
    ppermute x6 -> x3, waiting for transfers between devices: 6.45 us -> 1.19 us  [others(): lax.ppermute(value, 'ch', [(i, i ^ k) for i in range(lax.axis_size('ch'))])]
    ppermute x6 -> x3, starting transfers between devices: 4.72 us -> 2.22 us  [others(): lax.ppermute(value, 'ch', [(i, i ^ k) for i in range(lax.axis_size('ch'))])]
    unnamed x23 -> x14, local copies, waits for them, and re-layouts: 2.98 us -> 0.65 us
    pallas_call x4 -> x5, Pallas kernels: 5.67 us -> 6.31 us  [call(): pl.pallas_call(kernel, out_shape=outs, in_specs=[place] * len(inputs), ou...]
  transfers between devices with their start and end apart: 7 -> 4, of which waited for: 5 -> 3; matrix products, arithmetic and copies ran while one was open for 0% -> 0% of each run, Pallas kernels for 0% -> 1%
where the time goes in v1:
time: 46.5 us; the launch traced here: 46.2 us
  blocking collectives  22.7 us (49%)
  waiting for transfers between devices  10.4 us (22%)
  Pallas kernels  6.31 us (14%)
  starting transfers between devices  6.12 us (13%)
  local copies, waits for them, and re-layouts  0.65 us (1%)
    all_to_all x1, blocking collectives, exchange(): lax.all_to_all(value, ('sp', 'ch'), split_axis=0, concat_axis=0, tiled=True)  22.7 us
    all_to_all x1, waiting for transfers between devices, exchange(): lax.all_to_all(value, ('sp', 'ch'), split_axis=0, concat_axis=0, tiled=True)  9.17 us
    pallas_call x5, Pallas kernels, call(): pl.pallas_call(kernel, out_shape=outs, in_specs=[place] * len(inputs), ou...  6.31 us
    all_to_all x1, starting transfers between devices, exchange(): lax.all_to_all(value, ('sp', 'ch'), split_axis=0, concat_axis=0, tiled=True)  3.9 us
    ppermute x3, starting transfers between devices, others(): lax.ppermute(value, 'ch', [(i, i ^ k) for i in range(lax.axis_size('ch'))])  2.22 us
    ppermute x3, waiting for transfers between devices, others(): lax.ppermute(value, 'ch', [(i, i ^ k) for i in range(lax.axis_size('ch'))])  1.19 us
  transfers between devices with their start and end apart: 4, of which 3 were waited for; matrix products, arithmetic and copies ran while one was open for 0% of the time, Pallas kernels for 1%

profile of v1, /device:TPU:1, one launch (start us, length us, event | category | flops | bytes accessed | tf_op | source)
XLA Modules:
  0.0 46.2 jit_solution(6887839484688458912)
XLA Ops:
  0.0 1.2 %prep.1 = bf16[1024,128]{1,0:T(8,128)(2,1)S(1)} custom-call(bf16[128,128]{1,0:T(8,128)(2,1)} %bitcast.23, f32[9,64]{1,0:T(8,128)} %bitcast.24, f32[1,64]{1,0:T(1,128)} %bitcast.25, bf16[4,40,64]{2,1,0:T(8,128)(2,1)} %refs_3_.1, f32[4,8,64]{2,1,0:T(8,128)} %bitcast.18, f32[4,64]{1,0:T(4,128)} %dtb_ref.1, f32[4,16,64]{2,1,0:T(8,128)} %bitcast.16, f32[4,64]{1,0:T(4,128)} %skip_ref.1), custom_call_target="tpu_custom_call" | custom-call | tf_op jit(solution)/shard_map/prep/pallas_call | solution.py:391
  1.2 22.7 %all_to_all.22 = bf16[128,8,128]{2,1,0:T(8,128)(2,1)S(1)} all-to-all(bf16[128,8,128]{2,1,0:T(8,128)(2,1)S(1)} %bitcast.14), channel_id=1, replica_groups=mesh['sp'=32,'ch'=4] {'sp','ch'}, dimensions={0} | all-to-all | bytes 524288 | tf_op jit(solution)/shard_map/all_to_all | solution.py:410
  23.9 2.4 %columns.1 = bf16[512,128]{1,0:T(8,128)(2,1)} custom-call(bf16[1024,128]{1,0:T(8,128)(2,1)S(1)} %bitcast.13), custom_call_target="tpu_custom_call" | custom-call | tf_op jit(solution)/shard_map/columns/pallas_call | solution.py:391
  26.3 0.0 copy-start
  26.3 0.0 copy-start.1
  26.3 0.0 copy-start.2
  26.3 3.9 %all-to-all-start.1 = ((bf16[128,4,128]{2,1,0:T(4,128)(2,1)}), bf16[128,4,128]{2,1,0:T(4,128)(2,1)S(1)}, u32[]{:S(2)}, u32[]{:S(2)}) async-start(bf16[128,4,128]{2,1,0:T(4,128)(2,1)} %bitcast.7), calls=%async_computation.1 | async-start | bytes 262144 | tf_op jit(solution)/shard_map/all_to_all | solution.py:410
  30.2 0.0 copy-start.4
  30.2 0.0 copy-start.3
  30.2 0.0 copy-start.5
  30.3 0.0 copy-start.6
  30.3 0.0 copy-done
  30.3 0.0 copy-done.1
  30.3 0.0 copy-done.2
  30.3 0.6 %copy-done.4 = f32[4,64]{1,0:T(4,128)S(1)} copy-done((f32[4,64]{1,0:T(4,128)S(1)}, f32[4,64]{1,0:T(4,128)}, u32[]{:S(2)}) %copy-start.4) | copy-done | bytes 1048
  30.9 0.0 copy-done.3
  30.9 0.0 copy-done.5
  30.9 0.0 copy-done.6
  30.9 0.4 side.1
  31.4 9.2 %all-to-all-done.1 = bf16[128,4,128]{2,1,0:T(4,128)(2,1)S(1)} async-done(((bf16[128,4,128]{2,1,0:T(4,128)(2,1)}), bf16[128,4,128]{2,1,0:T(4,128)(2,1)S(1)}, u32[]{:S(2)}, u32[]{:S(2)}) %all-to-all-start.1) | async-done | bytes 131104 | tf_op jit(solution)/shard_map/all_to_all | solution.py:410
  40.5 1.6 %rows.1 = (f32[128,128]{1,0:T(8,128)S(1)}, f32[16,128]{1,0:T(8,128)S(1)}) custom-call(bf16[512,128]{1,0:T(8,128)(2,1)S(1)} %bitcast.15, f32[40,128]{1,0:T(8,128)S(1)} %get-tuple-element.12.vec_ref, bf16[256,256]{1,0:T(8,128)(2,1)S(1)} %get-tuple-element.13.high_ref, bf16[256,256]{1,0:T(8,128)(2,1)S(1)} %get-tuple-element.14.low_ref), custom_call_target="tpu_custom_call" | custom-call | tf_op jit(solution)/shard_map/rows/pallas_call | solution.py:391
  42.2 0.9 %collective-permute-start.2 = (f32[16,128]{1,0:T(8,128)S(1)}, f32[16,128]{1,0:T(8,128)S(1)}, u32[]{:S(2)}, u32[]{:S(2)}) collective-permute-start(f32[16,128]{1,0:T(8,128)S(1)} %get-tuple-element.16.refs_1_), channel_id=1, source_target_pairs={{0,3},{1,2},{2,1},{3,0},{4,7},{5,6},{6,5},{7,4},{8,11},{9,10},{10,... | collective-permute-start | bytes 24584 | tf_op jit(solution)/shard_map/ppermute | solution.py:404
  43.1 0.9 %collective-permute-start.1 = (f32[16,128]{1,0:T(8,128)S(1)}, f32[16,128]{1,0:T(8,128)S(1)}, u32[]{:S(2)}, u32[]{:S(2)}) collective-permute-start(f32[16,128]{1,0:T(8,128)S(1)} %get-tuple-element.16.refs_1_), channel_id=1, source_target_pairs={{0,2},{1,3},{2,0},{3,1},{4,6},{5,7},{6,4},{7,5},{8,10},{9,11},{10,... | collective-permute-start | bytes 24584 | tf_op jit(solution)/shard_map/ppermute | solution.py:404
  44.0 0.4 collective-permute-start
  44.4 0.9 %collective-permute-done.2.refs_4_ = f32[16,128]{1,0:T(8,128)S(1)} collective-permute-done((f32[16,128]{1,0:T(8,128)S(1)}, f32[16,128]{1,0:T(8,128)S(1)}, u32[]{:S(2)}, u32[]{:S(2)}) %collective-permute-start.2) | collective-permute-done | bytes 8224 | tf_op jit(solution)/shard_map/ppermute | solution.py:404
  45.3 0.3 collective-permute-done.1.refs_3_
  45.6 0.0 collective-permute-done.refs_2_
  45.6 0.6 %norm.1 = bf16[128,128]{1,0:T(8,128)(2,1)} custom-call(f32[128,128]{1,0:T(8,128)S(1)} %get-tuple-element.15.refs_0_, f32[16,128]{1,0:T(8,128)S(1)} %get-tuple-element.16.refs_1_, f32[16,128]{1,0:T(8,128)S(1)} %collective-permute-done.refs_2_, f32[16,128]{1,0:T(8,128)S(1)} %collective-permute-done.1.refs_3_, f32[16,128]{1,0:T(8,128)S(1)} %collective-permute-done.2.refs_4_, ...), custom_call_target="tpu_custom_call" | custom-call | tf_op jit(solution)/shard_map/norm/pallas_call | solution.py:391
Async XLA Ops:
  26.3 4.0 %copy-start = (f32[4,64,16]{1,2,0:T(8,128)S(1)}, f32[4,64,16]{1,2,0:T(8,128)}, u32[]{:S(2)}) copy-start(f32[4,64,16]{1,2,0:T(8,128)} %param.18) | copy-start | bytes 49156
  26.3 4.0 %copy-start.1 = (f32[4,64,8]{1,2,0:T(8,128)S(1)}, f32[4,64,8]{1,2,0:T(8,128)}, u32[]{:S(2)}) copy-start(f32[4,64,8]{1,2,0:T(8,128)} %param.16) | copy-start | bytes 24580
  26.3 4.0 %copy-start.2 = (bf16[64,2,128]{2,1,0:T(2,128)(2,1)S(1)}, bf16[64,2,128]{2,1,0:T(2,128)(2,1)}, u32[]{:S(2)}) copy-start(bf16[64,2,128]{2,1,0:T(2,128)(2,1)} %param.12) | copy-start | bytes 98308
  26.3 14.2 %all-to-all-start.1 = ((bf16[128,4,128]{2,1,0:T(4,128)(2,1)}), bf16[128,4,128]{2,1,0:T(4,128)(2,1)S(1)}, u32[]{:S(2)}, u32[]{:S(2)}) async-start(bf16[128,4,128]{2,1,0:T(4,128)(2,1)} %bitcast.7), calls=%async_computation.1 | async-start | bytes 262144 | tf_op jit(solution)/shard_map/all_to_all | solution.py:410
  30.2 0.7 %copy-start.4 = (f32[4,64]{1,0:T(4,128)S(1)}, f32[4,64]{1,0:T(4,128)}, u32[]{:S(2)}) copy-start(f32[4,64]{1,0:T(4,128)} %skip_ref.1) | copy-start | bytes 3076
  30.2 0.7 %copy-start.3 = (f32[4,64]{1,0:T(4,128)S(1)}, f32[4,64]{1,0:T(4,128)}, u32[]{:S(2)}) copy-start(f32[4,64]{1,0:T(4,128)} %dtb_ref.1) | copy-start | bytes 3076
  30.2 0.7 %copy-start.5 = (f32[64]{0:T(128)S(1)}, f32[64]{0:T(128)}, u32[]{:S(2)}) copy-start(f32[64]{0:T(128)} %param.20) | copy-start | bytes 772
  30.3 0.7 %copy-start.6 = (f32[64]{0:T(128)S(1)}, f32[64]{0:T(128)}, u32[]{:S(2)}) copy-start(f32[64]{0:T(128)} %param.21) | copy-start | bytes 772
  42.2 3.2 %collective-permute-start.2 = (f32[16,128]{1,0:T(8,128)S(1)}, f32[16,128]{1,0:T(8,128)S(1)}, u32[]{:S(2)}, u32[]{:S(2)}) collective-permute-start(f32[16,128]{1,0:T(8,128)S(1)} %get-tuple-element.16.refs_1_), channel_id=1, source_target_pairs={{0,3},{1,2},{2,1},{3,0},{4,7},{5,6},{6,5},{7,4},{8,11},{9,10},{10,... | collective-permute-start | bytes 24584 | tf_op jit(solution)/shard_map/ppermute | solution.py:404
  43.1 2.5 %collective-permute-start.1 = (f32[16,128]{1,0:T(8,128)S(1)}, f32[16,128]{1,0:T(8,128)S(1)}, u32[]{:S(2)}, u32[]{:S(2)}) collective-permute-start(f32[16,128]{1,0:T(8,128)S(1)} %get-tuple-element.16.refs_1_), channel_id=1, source_target_pairs={{0,2},{1,3},{2,0},{3,1},{4,6},{5,7},{6,4},{7,5},{8,10},{9,11},{10,... | collective-permute-start | bytes 24584 | tf_op jit(solution)/shard_map/ppermute | solution.py:404
  44.0 1.6 %collective-permute-start = (f32[16,128]{1,0:T(8,128)S(1)}, f32[16,128]{1,0:T(8,128)S(1)}, u32[]{:S(2)}, u32[]{:S(2)}) collective-permute-start(f32[16,128]{1,0:T(8,128)S(1)} %get-tuple-element.16.refs_1_), channel_id=1, source_target_pairs={{0,1},{1,0},{2,3},{3,2},{4,5},{5,4},{6,7},{7,6},{8,9},{9,8},{10,11... | collective-permute-start | bytes 24584 | tf_op jit(solution)/shard_map/ppermute | solution.py:404

commit v2 on v1

v2 whole, which is shorter than its diff:
```python
import math

import jax
import jax.numpy as jnp
from jax import lax
from jax.experimental import pallas as pl
from jax.experimental.pallas import tpu as pltpu
from jax.sharding import PartitionSpec as P

F32 = jnp.float32
BF16 = jnp.bfloat16
LANES = 128
EXACT = lax.Precision.HIGHEST
NEG_LOG2E = -1.0 / math.log(2.0)

CHUNK = 8
X_ROWS = 3
BACK = 6
PROJ_PAIRS = 80
VEC_PAIRS = 32


def iota(shape, axis):
    return lax.broadcasted_iota(jnp.int32, shape, axis)


def spread(chans, offset):
    lane = iota((chans, 2 * chans), 1)
    return jnp.where(lane == 2 * iota((chans, 2 * chans), 0) + offset, 1.0, 0.0).astype(F32)


def dup_rows(value, dup):
    return jnp.dot(value, dup, preferred_element_type=F32, precision=EXACT)


def softplus(x):
    return jnp.maximum(x, 0.0) + jnp.log1p(jnp.exp(-jnp.abs(x)))


def silu(x):
    return x * jax.nn.sigmoid(x)


def roll(x, shift, axis):
    return pltpu.roll(x, shift % x.shape[axis], axis)


def start_copies(sources, targets, arrived):
    copies = [
        pltpu.make_async_copy(source, target, arrived.at[index])
        for index, (source, target) in enumerate(zip(sources, targets))
    ]
    for copy in copies:
        copy.start()
    return copies


def prep_kernel(*refs):
    count = 8
    sources, send_ref, scr, vec, near, packed = refs[:count], *refs[count : count + 5]
    loaded, arrived = refs[count + 5 : -1], refs[-1]
    for copy in start_copies(sources, loaded, arrived):
        copy.wait()
    x_ref, cw_ref, cb_ref, pw_ref, dtw_ref, dtb_ref, rate_ref, skip_ref = loaded
    chans = cw_ref.shape[1]
    even, odd = spread(chans, 0), spread(chans, 1)
    even_b, odd_b = even.astype(BF16), odd.astype(BF16)
    half = VEC_PAIRS
    vec[0:9, :] = cw_ref[...]
    vec[9:10, :] = cb_ref[...]
    vec[10:12, :] = dtb_ref[2:4, :]
    vec[12:14, :] = skip_ref[2:4, :]
    vec[14:16, :] = jnp.zeros((2, chans), F32)
    vec[16:24, :] = dtw_ref[2]
    vec[24:32, :] = dtw_ref[3]
    vec[32:48, :] = rate_ref[2]
    vec[48:64, :] = rate_ref[3]
    high = vec[...].astype(BF16)
    low = (vec[0:half, :] - high[0:half].astype(F32)).astype(BF16)
    near[0:16, :] = rate_ref[0]
    near[16:24, :] = dtw_ref[0]
    near[24:25, :] = dtb_ref[0:1, :]
    near[25:26, :] = skip_ref[0:1, :] + skip_ref[1:2, :]
    near[26:32, :] = jnp.zeros((6, chans), F32)
    near[32:48, :] = rate_ref[1]
    near[48:56, :] = dtw_ref[1]
    near[56:57, :] = dtb_ref[1:2, :]
    near[57:64, :] = jnp.zeros((7, chans), F32)
    shared = near[...].astype(BF16)

    def pack(first, second):
        return jnp.dot(first, even_b, preferred_element_type=F32) + jnp.dot(
            second, odd_b, preferred_element_type=F32
        )

    third = pw_ref[2].astype(F32)
    fourth = pw_ref[3].astype(F32)
    rest = jnp.concatenate([third[0:8], fourth[0:8], third[8:40], fourth[8:40]], axis=0)
    packed[0:40, :] = pack(pw_ref[0], rest[0:40].astype(BF16))
    packed[40:80, :] = pack(pw_ref[1], rest[40:80].astype(BF16))
    packed[80:112, :] = pack(high[0:half], high[half:])
    packed[112:128, :] = pack(low[0:16], low[16:])
    packed[128:160, :] = pack(shared[0:half], shared[half:])

    turned = x_ref[...].astype(F32).T
    base = 2 * CHUNK
    scr[pl.ds(base + CHUNK, LANES, stride=CHUNK), :] = turned
    scr[pl.ds(base + 1, LANES, stride=CHUNK), :] = turned
    scr[pl.ds(base - CHUNK + 2, LANES, stride=CHUNK), :] = turned
    scr[base : base + 1, :] = jnp.zeros((1, LANES), F32)
    last = base + CHUNK * (LANES - 1) + 2
    scr[last : last + 1, :] = jnp.zeros((1, LANES), F32)
    slab = lax.axis_index("sp")
    for piece in range(CHUNK - X_ROWS):
        row = packed[pl.ds(32 * piece + slab, 1), :]
        scr[pl.ds(base + X_ROWS + piece, LANES, stride=CHUNK), :] = jnp.broadcast_to(row, (LANES, LANES))
    send_ref[...] = scr[base : base + CHUNK * LANES, :].astype(BF16)


def lane_rows(parts, columns, mask_ref, weights):
    shape = parts.shape
    picked = [
        parts * jnp.broadcast_to(mask_ref[j : j + 1, :], shape).astype(BF16) for j in columns
    ]
    return jnp.dot(jnp.concatenate(picked, axis=0), weights, preferred_element_type=F32)


def scan_pair(steps, rates, delta_ref, drive_ref, expand, wide_ref, part_ref, row_of):
    blocks = delta_ref.shape[1]
    states = [[jnp.zeros((16, LANES), F32) for _ in range(blocks)] for _ in range(2)]

    def prepare(turn):
        for way in range(2):
            first = 8 * turn if way == 0 else steps - 8 - 8 * turn
            for which in range(2):
                wide_ref[way, which, 16 * first : 16 * first + LANES, :] = expand(way, which, first)

    prepare(0)
    for step in range(steps):
        if step % 8 == 0 and step + 8 < steps:
            prepare(step // 8 + 1)
        for way in range(2):
            at = step if way == 0 else steps - 1 - step
            row = row_of(at)
            b_now, c_now = (wide_ref[way, which, 16 * at : 16 * at + 16, :] for which in range(2))
            for block in range(blocks):
                delta = delta_ref[way, block, row : row + 1, :]
                drive = drive_ref[way, block, row : row + 1, :]
                decay = jnp.exp2(delta * rates[way][block])
                state = decay * states[way][block] + drive * b_now
                states[way][block] = state
                product = c_now * state
                part_ref[way, block, 8 * row : 8 * row + 8, :] = product[0:8] + product[8:16]


def outputs_of(part_ref, block, half_ref):
    rows = part_ref.shape[2] // 8
    total = None
    for way in range(2):
        for lane_row in range(4):
            term = part_ref[way, block, pl.ds(lane_row, 2 * rows, stride=4), :]
            total = term if total is None else total + term
    half_ref[0 : 2 * rows, :] = total
    return half_ref[pl.ds(0, rows, stride=2), :] + half_ref[pl.ds(1, rows, stride=2), :]


def halves(value):
    high = value.astype(BF16)
    return high, (value - high.astype(F32)).astype(BF16)


def two_part_dot(value, high, low):
    return jnp.dot(value, high, preferred_element_type=F32) + jnp.dot(
        value, low, preferred_element_type=F32
    )


def row_weights(dtw_ref, dtb_ref, rate_ref, skip_ref, vec_ref, dup):
    for way in range(2):
        vec_ref[16 * way : 16 * way + 16, :] = dup_rows(rate_ref[way], dup) * NEG_LOG2E
        vec_ref[32 + 8 * way : 40 + 8 * way, :] = dup_rows(dtw_ref[way], dup)
    vec_ref[48:52, :] = dup_rows(dtb_ref[...], dup)
    skip = dup_rows(skip_ref[...], dup)
    vec_ref[52:53, :] = skip[0:1] + skip[1:2]
    vec_ref[53:56, :] = jnp.zeros((3, LANES), F32)


def step_weights(vec_refs):
    lane_row = iota((8, LANES), 1) % 2
    columns = []
    for ref in vec_refs:
        for way in range(2):
            dt_rows = ref[32 + 8 * way : 40 + 8 * way, :]
            column = []
            for row in range(2):
                column += [jnp.zeros((40 * way, LANES), F32)] if way else []
                column.append(jnp.where(lane_row == row, dt_rows, 0.0))
                column.append(jnp.zeros((LANES - 40 * way - 8, LANES), F32))
            columns.append(jnp.concatenate(column, axis=0))
    return halves(jnp.concatenate(columns, axis=1))


def column_kernel(recv_ref, *refs):
    count = 7
    sources, outputs = refs[:count], refs[count : count + 7]
    send_ref, own_ref, near_ref, high_ref, low_ref, gate_ref, affine_ref = outputs
    (
        flat_scr,
        back_scr,
        scr,
        delta_scr,
        drive_scr,
        part_scr,
        half_scr,
        mask_scr,
        wide_scr,
    ) = refs[count + 7 : count + 16]
    loaded, arrived = refs[count + 16 : -1], refs[-1]
    copies = start_copies(sources, loaded, arrived)
    slabs = LANES // 4
    pad = 8
    flat_scr[...] = recv_ref[...].astype(F32)
    for row in range(CHUNK):
        scr[row, pad - 4 : pad, :] = jnp.zeros((4, LANES), F32)
        scr[row, pad + LANES : pad + LANES + 4, :] = jnp.zeros((4, LANES), F32)
        scr[row, pad : pad + LANES, :] = flat_scr[pl.ds(row, LANES, stride=CHUNK), :]

    even = iota((slabs, LANES), 1) % 2 == 0
    vecs = []
    projs = []
    conv = []
    for group in range(4):

        def rows_of(row, shift):
            return scr[row, pl.ds(pad + group + 4 * shift, slabs, stride=4), :]

        pieces = [rows_of(row, 0) for row in range(X_ROWS, CHUNK)]
        projs.append([pieces[0], pieces[1], pieces[2][0:16]])
        low = pieces[3][16:32]
        even_16 = even[0:16]
        vec = jnp.concatenate(
            [
                pieces[2][16:32] + jnp.where(even_16, low, 0.0),
                pieces[3][0:16] + jnp.where(even_16, roll(low, -1, 1), 0.0),
            ],
            axis=0,
        )
        vecs.append(vec)
        taps = jnp.where(even[0:16], vec[0:16], roll(vec[0:16], 1, 1))
        total = jnp.zeros((slabs, LANES), F32) + taps[9:10, :]
        for side in range(3):
            here = rows_of(side, 0)
            up = jnp.where(even, roll(rows_of(side, -1), -1, 1), roll(here, 1, 1))
            down = jnp.where(even, roll(here, -1, 1), roll(rows_of(side, 1), 1, 1))
            total = total + taps[side : side + 1, :] * up
            total = total + taps[3 + side : 4 + side, :] * here
            total = total + taps[6 + side : 7 + side, :] * down
        conv.append(silu(total).astype(BF16).astype(F32))

    shared = scr[CHUNK - 1, pl.ds(pad + (lax.axis_index("ch") ^ 2), slabs, stride=4), :]
    for way, value in enumerate(
        (jnp.where(even, shared, roll(shared, 1, 1)), jnp.where(even, roll(shared, -1, 1), shared))
    ):
        near_ref[16 * way : 16 * way + 16, :] = value[0:16] * NEG_LOG2E
        near_ref[32 + 8 * way : 40 + 8 * way, :] = value[16:24]
        near_ref[48 + way : 49 + way, :] = value[24:25]
        if way == 0:
            near_ref[52:53, :] = value[25:26]
    near_ref[50:52, :] = jnp.zeros((2, LANES), F32)
    near_ref[53:56, :] = jnp.zeros((3, LANES), F32)

    def from_even(left, right):
        mask = iota(left.shape, 1) % 2 == 0
        return jnp.where(mask, left, roll(right, 1, 1))

    def from_odd(left, right):
        mask = iota(left.shape, 1) % 2 == 0
        return jnp.where(mask, roll(left, -1, 1), right)

    def all_groups(take, parts):
        return jnp.concatenate([take(parts[0], parts[1]), take(parts[2], parts[3])], axis=1)

    values = jnp.concatenate([all_groups(from_even, conv), all_groups(from_odd, conv)], axis=0)
    values_b = values.astype(BF16)
    proj_w = jnp.concatenate(
        [
            all_groups(take, [p[piece] for p in projs])
            for take in (from_even, from_odd)
            for piece in range(3)
        ],
        axis=0,
    ).astype(BF16)
    vec = jnp.concatenate([all_groups(from_even, vecs), all_groups(from_odd, vecs)], axis=0)

    nt = (((1,), (1,)), ((), ()))
    proj = lax.dot_general(values_b, proj_w[0:128], nt, preferred_element_type=F32)
    proj = proj.astype(BF16).astype(F32)
    turned = lax.dot_general(proj_w[96:160], values_b, nt, preferred_element_type=F32)
    turned = turned.astype(BF16)

    low = lax.dot_general(values_b, proj_w[80:96], nt, preferred_element_type=F32).astype(BF16)
    dt_rows = vec[16:32]
    second_half = iota((16, 256), 0) >= 8
    rates = []
    for way in range(2):
        chosen = jnp.where(second_half == (way == 1), dt_rows, 0.0)
        delta = softplus(two_part_dot(low, *halves(chosen)) + vec[10 + way : 11 + way, :])
        drive = delta * values
        scaled = vec[32 + 16 * way : 48 + 16 * way] * NEG_LOG2E
        rates.append([scaled[:, 0:LANES], scaled[:, LANES:]])
        for block in range(2):
            lanes = slice(LANES * block, LANES * block + LANES)
            delta_scr[way, block] = delta[:, lanes]
            drive_scr[way, block] = drive[:, lanes]

    def row_of(at):
        return (at % 2) * slabs + at // 2

    mask_scr[...] = jnp.where(iota((64, 64), 0) == iota((64, 64), 1), 1.0, 0.0)
    ones = jnp.ones((64, LANES), BF16)

    def expand(way, which, first):
        parts = turned[32 * way + 16 * which : 32 * way + 16 * which + 16]
        return lane_rows(parts, [row_of(first + j) for j in range(8)], mask_scr, ones)

    scan_pair(2 * slabs, rates, delta_scr, drive_scr, expand, wide_scr, part_scr, row_of)

    for copy in copies:
        copy.wait()
    dtw_ref, dtb_ref, rate_ref, skip_ref, gain_ref, bias_ref, gate_in_ref = loaded
    chans = dtw_ref.shape[2]
    dup = spread(chans, 0) + spread(chans, 1)
    row_weights(dtw_ref, dtb_ref, rate_ref, skip_ref, own_ref, dup)
    high_ref[...], low_ref[...] = step_weights((own_ref, near_ref))
    gate_ref[...] = silu(gate_in_ref[...].astype(F32))
    pick = iota((LANES, LANES), 0) == iota((LANES, LANES), 1)
    for index, ref in enumerate((gain_ref, bias_ref)):
        column = jnp.sum(jnp.where(pick, dup_rows(ref[...], dup), 0.0), axis=1, keepdims=True)
        affine_ref[index] = jnp.broadcast_to(column, (LANES, LANES))

    skip = vec[12:13] + vec[13:14]
    backs = []
    for block in range(2):
        lanes = slice(LANES * block, LANES * block + LANES)
        y = outputs_of(part_scr, block, half_scr) + skip[:, lanes] * values[:, lanes]
        y_even, y_odd = y[0:slabs], y[slabs:]
        backs.append(jnp.where(even, y_even, roll(y_odd, 1, 1)))
        backs.append(jnp.where(even, roll(y_even, -1, 1), y_odd))
    for group in range(4):
        near = group ^ 2
        parts = (backs[group], conv[group], proj[0:slabs], proj[slabs:], backs[near], conv[near])
        for row, value in enumerate(parts):
            scr[row, pl.ds(group, slabs, stride=4), :] = value
    for row in range(BACK):
        back_scr[pl.ds(row, LANES, stride=BACK), :] = scr[row, 0:LANES, :]
    send_ref[...] = back_scr[...].astype(BF16)


def row_kernel(
    recv_ref,
    own_ref,
    near_ref,
    high_ref,
    low_ref,
    comb_ref,
    sums_ref,
    scr,
    mixed_scr,
    delta_scr,
    drive_scr,
    part_scr,
    half_scr,
    mask_scr,
    wide_scr,
):
    cols = LANES
    scr[...] = recv_ref[...].astype(F32)

    def chunk_row(row):
        return scr[pl.ds(row, cols, stride=BACK), :]

    proj = [chunk_row(2), chunk_row(3)]
    both = jnp.concatenate(proj, axis=1).astype(BF16)
    low_rank = two_part_dot(both, high_ref[...], low_ref[...])
    vecs = (own_ref, near_ref)
    verticals = (chunk_row(0), chunk_row(4))
    values = (chunk_row(1), chunk_row(5))
    for block in range(2):
        for way in range(2):
            first = LANES * (2 * block + way)
            delta = softplus(
                low_rank[:, first : first + LANES] + vecs[block][48 + way : 49 + way, :]
            )
            delta_scr[way, block] = delta
            drive_scr[way, block] = delta * values[block]
    rates = [[vec[16 * way : 16 * way + 16, :] for vec in vecs] for way in range(2)]

    for row in range(2):
        mixed_scr[pl.ds(row, cols, stride=2), :] = proj[row]
    turned = mixed_scr[...].T
    mask_scr[...] = jnp.where(iota((64, LANES), 1) // 2 == iota((64, LANES), 0), 1.0, 0.0)
    alike = iota((LANES, LANES), 0) % 2 == iota((LANES, LANES), 1) % 2
    by_row = jnp.where(alike, 1.0, 0.0).astype(BF16)

    def expand(way, which, first):
        top = 40 * way + 8 + 16 * which
        start = LANES * (first // 64)
        parts = turned[top : top + 16, start : start + LANES].astype(BF16)
        return lane_rows(parts, [(first + j) % 64 for j in range(8)], mask_scr, by_row)

    scan_pair(cols, rates, delta_scr, drive_scr, expand, wide_scr, part_scr, lambda at: at)
    sums = [jnp.zeros((8, LANES), F32) for _ in range(2)]
    for block in range(2):
        combined = (
            outputs_of(part_scr, block, half_scr)
            + vecs[block][52:53, :] * values[block]
            + verticals[block]
        )
        combined = combined.T
        if block == 0:
            comb_ref[...] = combined
        for tile in range(LANES // 8):
            rows = combined[8 * tile : 8 * tile + 8]
            sums = [sums[0] + rows, sums[1] + rows * rows]
    for index, value in enumerate(sums):
        value = value + roll(value, 4, 0)
        value = value + roll(value, 2, 0)
        sums_ref[8 * index : 8 * index + 8, :] = value


def norm_kernel(total_chans, comb_ref, s0_ref, s1_ref, gate_ref, affine_ref, out_ref):
    sums = s0_ref[...] + s1_ref[...]
    mean = sums[0:8] / total_chans
    var = sums[8:16] / total_chans - mean * mean
    scale = lax.rsqrt(var + 1e-05)
    comb = comb_ref[...]
    means = jnp.concatenate([mean] * (LANES // 8), axis=0)
    scales = jnp.concatenate([scale] * (LANES // 8), axis=0)
    normed = (comb - means) * scales * affine_ref[0] + affine_ref[1]
    out_ref[...] = (normed * gate_ref[...]).astype(BF16)


VMEM = pl.BlockSpec(memory_space=pltpu.VMEM)


def call(kernel, name, outs, scratch, inputs, place=VMEM, grant=24 << 20):
    single = not isinstance(outs, (list, tuple))
    return pl.pallas_call(
        kernel,
        out_shape=outs,
        in_specs=place if isinstance(place, list) else [place] * len(inputs),
        out_specs=VMEM if single else [VMEM] * len(outs),
        scratch_shapes=scratch,
        name=name,
        compiler_params=pltpu.CompilerParams(vmem_limit_bytes=grant),
    )(*inputs)


def other(value, flip):
    return lax.ppermute(value, "ch", [(i, i ^ flip) for i in range(lax.axis_size("ch"))])


def exchange(value, chunk, tile):
    peers = value.shape[0] // chunk
    pieces = value.reshape(peers, chunk // tile, tile, LANES)
    moved = lax.all_to_all(pieces, ("sp", "ch"), split_axis=0, concat_axis=0, tiled=True)
    return moved.reshape(value.shape)


def on_device(
    x_in,
    gate_in,
    conv_weight,
    conv_bias,
    proj_weight,
    dt_weight,
    dt_bias,
    decay_rate,
    skip_gain,
    norm_gain,
    norm_bias,
):
    chans, rows, cols = x_in.shape
    total_chans = chans * lax.axis_size("ch")
    flat = (chans * rows, cols)
    struct = jax.ShapeDtypeStruct

    def vm(*shape):
        return pltpu.VMEM(shape, F32)

    dt_weight = dt_weight.transpose(0, 2, 1)
    decay_rate = decay_rate.transpose(0, 2, 1)
    arguments = [
        x_in.reshape(flat),
        conv_weight.T,
        conv_bias.reshape(1, chans),
        proj_weight,
        dt_weight,
        dt_bias,
        decay_rate,
        skip_gain,
    ]
    send = call(
        prep_kernel,
        "prep",
        struct((CHUNK * cols, LANES), BF16),
        [vm(CHUNK * (cols + 4), LANES), vm(2 * VEC_PAIRS, chans), vm(64, chans), vm(160, LANES)]
        + [pltpu.VMEM(value.shape, value.dtype) for value in arguments]
        + [pltpu.SemaphoreType.DMA((len(arguments),))],
        [pltpu.with_memory_space_constraint(value, pltpu.HBM) for value in arguments],
        pl.BlockSpec(memory_space=pltpu.HBM),
    )
    hbm = pl.BlockSpec(memory_space=pltpu.HBM)
    arguments = [
        pltpu.with_memory_space_constraint(value, pltpu.HBM)
        for value in (
            dt_weight,
            dt_bias,
            decay_rate,
            skip_gain,
            norm_gain.reshape(1, chans),
            norm_bias.reshape(1, chans),
            gate_in.reshape(flat),
        )
    ]
    send, own, near, high, low, gate, affine = call(
        column_kernel,
        "columns",
        [
            struct((BACK * cols, LANES), BF16),
            struct((56, LANES), F32),
            struct((56, LANES), F32),
            struct((2 * LANES, 4 * LANES), BF16),
            struct((2 * LANES, 4 * LANES), BF16),
            struct((LANES, cols), F32),
            struct((2, LANES, cols), F32),
        ],
        [
            vm(CHUNK * cols, LANES),
            vm(BACK * cols, LANES),
            vm(CHUNK, cols + 16, LANES),
            vm(2, 2, 64, LANES),
            vm(2, 2, 64, LANES),
            vm(2, 2, 8 * 64, LANES),
            vm(LANES, LANES),
            vm(64, 64),
            vm(2, 2, 16 * 64, LANES),
        ]
        + [pltpu.VMEM(value.shape, value.dtype) for value in arguments]
        + [pltpu.SemaphoreType.DMA((len(arguments),))],
        [exchange(send, CHUNK, CHUNK)] + arguments,
        [VMEM] + [hbm] * len(arguments),
    )
    received = exchange(send, BACK, 2)
    combined, sums = call(
        row_kernel,
        "rows",
        [struct((LANES, cols), F32), struct((16, cols), F32)],
        [
            vm(BACK * cols, LANES),
            vm(2 * cols, LANES),
            vm(2, 2, cols, LANES),
            vm(2, 2, cols, LANES),
            vm(2, 2, 8 * cols, LANES),
            vm(2 * cols, LANES),
            vm(64, LANES),
            vm(2, 2, 16 * cols, LANES),
        ],
        [received, own, near, high, low],
    )
    out = call(
        lambda *refs: norm_kernel(total_chans, *refs),
        "norm",
        struct(flat, BF16),
        [],
        [combined, sums, other(sums, 1), gate, affine],
    )
    return out.reshape(chans, rows, cols)


def solution(mesh):
    placed = (
        P("ch", "sp", None),
        P("ch", "sp", None),
        P("ch", None),
        P("ch"),
        P(None, None, "ch"),
        P(None, "ch", None),
        P(None, "ch"),
        P(None, "ch", None),
        P(None, "ch"),
        P("ch"),
        P("ch"),
    )
    return jax.shard_map(
        on_device, mesh=mesh, in_specs=placed, out_specs=P("ch", "sp", None), check_vma=False
    )
```

time: 46.5 us -> 44.2 us (0.951)
  blocking collectives: 22.7 us -> 37.2 us
  waiting for transfers between devices: 10.4 us -> 0.83 us
  starting transfers between devices: 6.12 us -> 0.47 us
  Pallas kernels: 6.31 us -> 5.55 us
  local copies, waits for them, and re-layouts: 0.65 us -> 0 us
    all_to_all x1 -> x2, blocking collectives: 22.7 us -> 37.2 us  [exchange(): lax.all_to_all(pieces, ('sp', 'ch'), split_axis=0, concat_axis=0, tiled=T...]
    all_to_all x1 -> x0, waiting for transfers between devices: 9.17 us -> none  [exchange(): lax.all_to_all(value, ('sp', 'ch'), split_axis=0, concat_axis=0, tiled=True)]
    all_to_all x1 -> x0, starting transfers between devices: 3.9 us -> none  [exchange(): lax.all_to_all(value, ('sp', 'ch'), split_axis=0, concat_axis=0, tiled=True)]
    ppermute x3 -> x1, starting transfers between devices: 2.22 us -> 0.47 us  [other(): lax.ppermute(value, 'ch', [(i, i ^ flip) for i in range(lax.axis_size('ch...]
    pallas_call x5 -> x4, Pallas kernels: 6.31 us -> 5.55 us  [call(): pl.pallas_call(kernel, out_shape=outs, in_specs=place if isinstance(place...]
    unnamed x14 -> x0, local copies, waits for them, and re-layouts: 0.65 us -> none
    ppermute x3 -> x1, waiting for transfers between devices: 1.19 us -> 0.83 us  [other(): lax.ppermute(value, 'ch', [(i, i ^ flip) for i in range(lax.axis_size('ch...]
  transfers between devices with their start and end apart: 4 -> 1, of which waited for: 3 -> 1; matrix products, arithmetic and copies ran while one was open for 0% -> 0% of each run, Pallas kernels for 1% -> 0%
where the time goes in v2:
time: 44.2 us; the launch traced here: 44 us
  blocking collectives  37.2 us (84%)
  Pallas kernels  5.55 us (13%)
  waiting for transfers between devices  0.83 us (2%)
  starting transfers between devices  0.47 us (1%)
    all_to_all x2, blocking collectives, exchange(): lax.all_to_all(pieces, ('sp', 'ch'), split_axis=0, concat_axis=0, tiled=T...  37.2 us
    pallas_call x4, Pallas kernels, call(): pl.pallas_call(kernel, out_shape=outs, in_specs=place if isinstance(place...  5.55 us
  transfers between devices with their start and end apart: 1, of which 1 were waited for; matrix products, arithmetic and copies ran while one was open for 0% of the time, Pallas kernels for 0%

profile of v2, /device:TPU:1, one launch (start us, length us, event | category | flops | bytes accessed | tf_op | source)
XLA Modules:
  0.0 44.0 jit_solution(7949440702587778104)
XLA Ops:
  0.0 1.2 %prep.1 = bf16[1024,128]{1,0:T(8,128)(2,1)S(1)} custom-call(bf16[128,128]{1,0:T(8,128)(2,1)} %bitcast.23, f32[9,64]{1,0:T(8,128)} %bitcast.25, f32[1,64]{1,0:T(1,128)} %bitcast.26, bf16[4,40,64]{2,1,0:T(8,128)(2,1)} %refs_3_.2, f32[4,8,64]{2,1,0:T(8,128)} %bitcast.21, f32[4,64]{1,0:T(4,128)} %refs_1_.1, f32[4,16,64]{2,1,0:T(8,128)} %bitcast.19, f32[4,64]{1,0:T(4,128)} %refs_3_.3), custom_call_target="tpu_custom_call" | custom-call | tf_op jit(solution)/shard_map/prep/pallas_call | solution.py:448
  1.2 22.7 %all_to_all.10 = bf16[128,1,8,128]{3,2,1,0:T(8,128)(2,1)S(1)} all-to-all(bf16[128,1,8,128]{3,2,1,0:T(8,128)(2,1)S(1)} %bitcast.16), channel_id=1, replica_groups=mesh['sp'=32,'ch'=4] {'sp','ch'}, dimensions={0} | all-to-all | bytes 524288 | tf_op jit(solution)/shard_map/all_to_all | solution.py:466
  23.9 1.9 %columns.1 = (bf16[768,128]{1,0:T(8,128)(2,1)S(1)}, f32[56,128]{1,0:T(8,128)S(1)}, f32[56,128]{1,0:T(8,128)S(1)}, bf16[256,512]{1,0:T(8,128)(2,1)S(1)}, bf16[256...) custom-call(bf16[1024,128]{1,0:T(8,128)(2,1)S(1)} %bitcast.15, f32[4,8,64]{2,1,0:T(8,128)} %bitcast.22, ...), custom_call_target="tpu_custom_call" | custom-call | tf_op jit(solution)/shard_map/columns/pallas_call | solution.py:448
  25.8 14.5 %all_to_all.11 = bf16[128,3,2,128]{3,2,1,0:T(2,128)(2,1)S(1)} all-to-all(bf16[128,3,2,128]{3,2,1,0:T(2,128)(2,1)S(1)} %bitcast.18), channel_id=1, replica_groups=mesh['sp'=32,'ch'=4] {'sp','ch'}, dimensions={0} | all-to-all | bytes 393216 | tf_op jit(solution)/shard_map/all_to_all | solution.py:466
  40.3 1.8 %rows.1 = (f32[128,128]{1,0:T(8,128)S(1)}, f32[16,128]{1,0:T(8,128)S(1)}) custom-call(bf16[768,128]{1,0:T(8,128)(2,1)S(1)} %bitcast.17, f32[56,128]{1,0:T(8,128)S(1)} %get-tuple-element.15.own_ref, f32[56,128]{1,0:T(8,128)S(1)} %get-tuple-element.16.near_ref, bf16[256,512]{1,0:T(8,128)(2,1)S(1)} %get-tuple-element.17.high_ref, ...), custom_call_target="tpu_custom_call" | custom-call | tf_op jit(solution)/shard_map/rows/pallas_call | solution.py:448
  42.1 0.5 %collective-permute-start = (f32[16,128]{1,0:T(8,128)S(1)}, f32[16,128]{1,0:T(8,128)S(1)}, u32[]{:S(2)}, u32[]{:S(2)}) collective-permute-start(f32[16,128]{1,0:T(8,128)S(1)} %get-tuple-element.20.refs_1_), channel_id=1, source_target_pairs={{0,1},{1,0},{2,3},{3,2},{4,5},{5,4},{6,7},{7,6},{8,9},{9,8},{10,11... | collective-permute-start | bytes 24584 | tf_op jit(solution)/shard_map/ppermute | solution.py:460
  42.6 0.8 %collective-permute-done.refs_2_ = f32[16,128]{1,0:T(8,128)S(1)} collective-permute-done((f32[16,128]{1,0:T(8,128)S(1)}, f32[16,128]{1,0:T(8,128)S(1)}, u32[]{:S(2)}, u32[]{:S(2)}) %collective-permute-start) | collective-permute-done | bytes 8224 | tf_op jit(solution)/shard_map/ppermute | solution.py:460
  43.4 0.6 %norm.1 = bf16[128,128]{1,0:T(8,128)(2,1)} custom-call(f32[128,128]{1,0:T(8,128)S(1)} %get-tuple-element.19.refs_0_, f32[16,128]{1,0:T(8,128)S(1)} %get-tuple-element.20.refs_1_, f32[16,128]{1,0:T(8,128)S(1)} %collective-permute-done.refs_2_, f32[128,128]{1,0:T(8,128)S(1)} %get-tuple-element.21.refs_3_, f32[2,128,128]{2,1,0:T(8,128)S(1)} %get-tuple-element.22.refs_4_), custom_call_target="tpu_custom_call" | custom-call | tf_op jit(solution)/shard_map/norm/pallas_call | solution.py:448
Async XLA Ops:
  42.1 1.3 %collective-permute-start = (f32[16,128]{1,0:T(8,128)S(1)}, f32[16,128]{1,0:T(8,128)S(1)}, u32[]{:S(2)}, u32[]{:S(2)}) collective-permute-start(f32[16,128]{1,0:T(8,128)S(1)} %get-tuple-element.20.refs_1_), channel_id=1, source_target_pairs={{0,1},{1,0},{2,3},{3,2},{4,5},{5,4},{6,7},{7,6},{8,9},{9,8},{10,11... | collective-permute-start | bytes 24584 | tf_op jit(solution)/shard_map/ppermute | solution.py:460

commit v3 on v2

--- a/solution.py
+++ b/solution.py
@@ -34,7 +34,7 @@
 
 
 def softplus(x):
-    return jnp.maximum(x, 0.0) + jnp.log1p(jnp.exp(-jnp.abs(x)))
+    return jnp.maximum(x, 0.0) + jnp.log(1.0 + jnp.exp(-jnp.abs(x)))
 
 
 def silu(x):
@@ -56,12 +56,20 @@
 
 
 def prep_kernel(*refs):
-    count = 8
-    sources, send_ref, scr, vec, near, packed = refs[:count], *refs[count : count + 5]
-    loaded, arrived = refs[count + 5 : -1], refs[-1]
-    for copy in start_copies(sources, loaded, arrived):
+    count, kept = 11, 7
+    sources, send_ref, col_mask_ref, row_mask_ref = refs[:count], *refs[count : count + 3]
+    handed = refs[count + 3 : count + 3 + kept]
+    scr, vec, near, packed, *own, arrived = refs[count + 3 + kept :]
+    loaded = (*own, *handed)
+    copies = start_copies(sources, loaded, arrived)
+    for j in range(64):
+        rows = slice(16 * j, 16 * j + 16)
+        lane = iota((16, LANES), 1)
+        col_mask_ref[rows, :] = jnp.where(lane[:, 0:64] == j, 1.0, 0.0).astype(BF16)
+        row_mask_ref[rows, :] = jnp.where(lane // 2 == j, 1.0, 0.0).astype(BF16)
+    for copy in copies:
         copy.wait()
-    x_ref, cw_ref, cb_ref, pw_ref, dtw_ref, dtb_ref, rate_ref, skip_ref = loaded
+    x_ref, cw_ref, cb_ref, pw_ref, dtw_ref, dtb_ref, rate_ref, skip_ref = loaded[:8]
     chans = cw_ref.shape[1]
     even, odd = spread(chans, 0), spread(chans, 1)
     even_b, odd_b = even.astype(BF16), odd.astype(BF16)
@@ -118,10 +126,7 @@
 
 
 def lane_rows(parts, columns, mask_ref, weights):
-    shape = parts.shape
-    picked = [
-        parts * jnp.broadcast_to(mask_ref[j : j + 1, :], shape).astype(BF16) for j in columns
-    ]
+    picked = [parts * mask_ref[16 * j : 16 * j + 16, :] for j in columns]
     return jnp.dot(jnp.concatenate(picked, axis=0), weights, preferred_element_type=F32)
 
 
@@ -200,30 +205,46 @@
     return halves(jnp.concatenate(columns, axis=1))
 
 
-def column_kernel(recv_ref, *refs):
-    count = 7
-    sources, outputs = refs[:count], refs[count : count + 7]
-    send_ref, own_ref, near_ref, high_ref, low_ref, gate_ref, affine_ref = outputs
-    (
-        flat_scr,
-        back_scr,
-        scr,
-        delta_scr,
-        drive_scr,
-        part_scr,
-        half_scr,
-        mask_scr,
-        wide_scr,
-    ) = refs[count + 7 : count + 16]
-    loaded, arrived = refs[count + 16 : -1], refs[-1]
-    copies = start_copies(sources, loaded, arrived)
+def column_kernel(
+    recv_ref,
+    mask_ref,
+    dtw_ref,
+    dtb_ref,
+    rate_ref,
+    skip_ref,
+    gain_ref,
+    bias_ref,
+    gate_in_ref,
+    send_ref,
+    own_ref,
+    near_ref,
+    high_ref,
+    low_ref,
+    gate_ref,
+    affine_ref,
+    flat_scr,
+    back_scr,
+    scr,
+    swap_scr,
+    delta_scr,
+    drive_scr,
+    part_scr,
+    half_scr,
+    wide_scr,
+):
     slabs = LANES // 4
     pad = 8
     flat_scr[...] = recv_ref[...].astype(F32)
+    swapped = iota((LANES, LANES), 1) ^ 1
     for row in range(CHUNK):
-        scr[row, pad - 4 : pad, :] = jnp.zeros((4, LANES), F32)
-        scr[row, pad + LANES : pad + LANES + 4, :] = jnp.zeros((4, LANES), F32)
-        scr[row, pad : pad + LANES, :] = flat_scr[pl.ds(row, LANES, stride=CHUNK), :]
+        value = flat_scr[pl.ds(row, LANES, stride=CHUNK), :]
+        scr[row] = value
+        if row < X_ROWS:
+            swap_scr[row, pad - 4 : pad, :] = jnp.zeros((4, LANES), F32)
+            swap_scr[row, pad + LANES : pad + LANES + 4, :] = jnp.zeros((4, LANES), F32)
+            swap_scr[row, pad : pad + LANES, :] = jnp.take_along_axis(
+                value, swapped, axis=1, mode="promise_in_bounds"
+            )
 
     even = iota((slabs, LANES), 1) % 2 == 0
     vecs = []
@@ -231,10 +252,13 @@
     conv = []
     for group in range(4):
 
-        def rows_of(row, shift):
-            return scr[row, pl.ds(pad + group + 4 * shift, slabs, stride=4), :]
-
-        pieces = [rows_of(row, 0) for row in range(X_ROWS, CHUNK)]
+        def rows_of(row):
+            return scr[row, pl.ds(group, slabs, stride=4), :]
+
+        def swapped_of(row, shift):
+            return swap_scr[row, pl.ds(pad + group + 4 * shift, slabs, stride=4), :]
+
+        pieces = [rows_of(row) for row in range(X_ROWS, CHUNK)]
         projs.append([pieces[0], pieces[1], pieces[2][0:16]])
         low = pieces[3][16:32]
         even_16 = even[0:16]
@@ -249,15 +273,14 @@
         taps = jnp.where(even[0:16], vec[0:16], roll(vec[0:16], 1, 1))
         total = jnp.zeros((slabs, LANES), F32) + taps[9:10, :]
         for side in range(3):
-            here = rows_of(side, 0)
-            up = jnp.where(even, roll(rows_of(side, -1), -1, 1), roll(here, 1, 1))
-            down = jnp.where(even, roll(here, -1, 1), roll(rows_of(side, 1), 1, 1))
-            total = total + taps[side : side + 1, :] * up
-            total = total + taps[3 + side : 4 + side, :] * here
-            total = total + taps[6 + side : 7 + side, :] * down
+            above, below = taps[side : side + 1, :], taps[6 + side : 7 + side, :]
+            beyond = jnp.where(even, swapped_of(side, -1), swapped_of(side, 1))
+            total = total + jnp.where(even[0:1], above, below) * beyond
+            total = total + jnp.where(even[0:1], below, above) * swapped_of(side, 0)
+            total = total + taps[3 + side : 4 + side, :] * rows_of(side)
         conv.append(silu(total).astype(BF16).astype(F32))
 
-    shared = scr[CHUNK - 1, pl.ds(pad + (lax.axis_index("ch") ^ 2), slabs, stride=4), :]
+    shared = scr[CHUNK - 1, pl.ds(lax.axis_index("ch") ^ 2, slabs, stride=4), :]
     for way, value in enumerate(
         (jnp.where(even, shared, roll(shared, 1, 1)), jnp.where(even, roll(shared, -1, 1), shared))
     ):
@@ -268,6 +291,16 @@
             near_ref[52:53, :] = value[25:26]
     near_ref[50:52, :] = jnp.zeros((2, LANES), F32)
     near_ref[53:56, :] = jnp.zeros((3, LANES), F32)
+
+    chans = dtw_ref.shape[2]
+    dup = spread(chans, 0) + spread(chans, 1)
+    row_weights(dtw_ref, dtb_ref, rate_ref, skip_ref, own_ref, dup)
+    high_ref[...], low_ref[...] = step_weights((own_ref, near_ref))
+    gate_ref[...] = silu(gate_in_ref[...].astype(F32))
+    pick = iota((LANES, LANES), 0) == iota((LANES, LANES), 1)
+    for index, ref in enumerate((gain_ref, bias_ref)):
+        column = jnp.sum(jnp.where(pick, dup_rows(ref[...], dup), 0.0), axis=1, keepdims=True)
+        affine_ref[index] = jnp.broadcast_to(column, (LANES, LANES))
 
     def from_even(left, right):
         mask = iota(left.shape, 1) % 2 == 0
@@ -316,27 +349,13 @@
     def row_of(at):
         return (at % 2) * slabs + at // 2
 
-    mask_scr[...] = jnp.where(iota((64, 64), 0) == iota((64, 64), 1), 1.0, 0.0)
     ones = jnp.ones((64, LANES), BF16)
 
     def expand(way, which, first):
         parts = turned[32 * way + 16 * which : 32 * way + 16 * which + 16]
-        return lane_rows(parts, [row_of(first + j) for j in range(8)], mask_scr, ones)
+        return lane_rows(parts, [row_of(first + j) for j in range(8)], mask_ref, ones)
 
     scan_pair(2 * slabs, rates, delta_scr, drive_scr, expand, wide_scr, part_scr, row_of)
-
-    for copy in copies:
-        copy.wait()
-    dtw_ref, dtb_ref, rate_ref, skip_ref, gain_ref, bias_ref, gate_in_ref = loaded
-    chans = dtw_ref.shape[2]
-    dup = spread(chans, 0) + spread(chans, 1)
-    row_weights(dtw_ref, dtb_ref, rate_ref, skip_ref, own_ref, dup)
-    high_ref[...], low_ref[...] = step_weights((own_ref, near_ref))
-    gate_ref[...] = silu(gate_in_ref[...].astype(F32))
-    pick = iota((LANES, LANES), 0) == iota((LANES, LANES), 1)
-    for index, ref in enumerate((gain_ref, bias_ref)):
-        column = jnp.sum(jnp.where(pick, dup_rows(ref[...], dup), 0.0), axis=1, keepdims=True)
-        affine_ref[index] = jnp.broadcast_to(column, (LANES, LANES))
 
     skip = vec[12:13] + vec[13:14]
     backs = []
@@ -358,6 +377,7 @@
 
 def row_kernel(
     recv_ref,
+    mask_ref,
     own_ref,
     near_ref,
     high_ref,
@@ -370,7 +390,6 @@
     drive_scr,
     part_scr,
     half_scr,
-    mask_scr,
     wide_scr,
 ):
     cols = LANES
@@ -398,7 +417,6 @@
     for row in range(2):
         mixed_scr[pl.ds(row, cols, stride=2), :] = proj[row]
     turned = mixed_scr[...].T
-    mask_scr[...] = jnp.where(iota((64, LANES), 1) // 2 == iota((64, LANES), 0), 1.0, 0.0)
     alike = iota((LANES, LANES), 0) % 2 == iota((LANES, LANES), 1) % 2
     by_row = jnp.where(alike, 1.0, 0.0).astype(BF16)
 
@@ -406,7 +424,7 @@
         top = 40 * way + 8 + 16 * which
         start = LANES * (first // 64)
         parts = turned[top : top + 16, start : start + LANES].astype(BF16)
-        return lane_rows(parts, [(first + j) % 64 for j in range(8)], mask_scr, by_row)
+        return lane_rows(parts, [(first + j) % 64 for j in range(8)], mask_ref, by_row)
 
     scan_pair(cols, rates, delta_scr, drive_scr, expand, wide_scr, part_scr, lambda at: at)
     sums = [jnp.zeros((8, LANES), F32) for _ in range(2)]
@@ -448,7 +466,7 @@
     return pl.pallas_call(
         kernel,
         out_shape=outs,
-        in_specs=place if isinstance(place, list) else [place] * len(inputs),
+        in_specs=[place] * len(inputs),
         out_specs=VMEM if single else [VMEM] * len(outs),
         scratch_shapes=scratch,
         name=name,
@@ -491,29 +509,12 @@
     dt_weight = dt_weight.transpose(0, 2, 1)
     decay_rate = decay_rate.transpose(0, 2, 1)
     arguments = [
-        x_in.reshape(flat),
-        conv_weight.T,
-        conv_bias.reshape(1, chans),
-        proj_weight,
-        dt_weight,
-        dt_bias,
-        decay_rate,
-        skip_gain,
-    ]
-    send = call(
-        prep_kernel,
-        "prep",
-        struct((CHUNK * cols, LANES), BF16),
-        [vm(CHUNK * (cols + 4), LANES), vm(2 * VEC_PAIRS, chans), vm(64, chans), vm(160, LANES)]
-        + [pltpu.VMEM(value.shape, value.dtype) for value in arguments]
-        + [pltpu.SemaphoreType.DMA((len(arguments),))],
-        [pltpu.with_memory_space_constraint(value, pltpu.HBM) for value in arguments],
-        pl.BlockSpec(memory_space=pltpu.HBM),
-    )
-    hbm = pl.BlockSpec(memory_space=pltpu.HBM)
-    arguments = [
         pltpu.with_memory_space_constraint(value, pltpu.HBM)
         for value in (
+            x_in.reshape(flat),
+            conv_weight.T,
+            conv_bias.reshape(1, chans),
+            proj_weight,
             dt_weight,
             dt_bias,
             decay_rate,
@@ -523,6 +524,26 @@
             gate_in.reshape(flat),
         )
     ]
+    send, col_mask, row_mask, *handed = call(
+        prep_kernel,
+        "prep",
+        [
+            struct((CHUNK * cols, LANES), BF16),
+            struct((64 * 16, 64), BF16),
+            struct((64 * 16, LANES), BF16),
+        ]
+        + [struct(value.shape, value.dtype) for value in arguments[4:]],
+        [
+            vm(CHUNK * (cols + 4), LANES),
+            vm(2 * VEC_PAIRS, chans),
+            vm(64, chans),
+            vm(160, LANES),
+        ]
+        + [pltpu.VMEM(value.shape, value.dtype) for value in arguments[:4]]
+        + [pltpu.SemaphoreType.DMA((len(arguments),))],
+        arguments,
+        pl.BlockSpec(memory_space=pltpu.HBM),
+    )
     send, own, near, high, low, gate, affine = call(
         column_kernel,
         "columns",
@@ -538,18 +559,15 @@
         [
             vm(CHUNK * cols, LANES),
             vm(BACK * cols, LANES),
-            vm(CHUNK, cols + 16, LANES),
+            vm(CHUNK, cols, LANES),
+            vm(X_ROWS, cols + 16, LANES),
             vm(2, 2, 64, LANES),
             vm(2, 2, 64, LANES),
             vm(2, 2, 8 * 64, LANES),
             vm(LANES, LANES),
-            vm(64, 64),
             vm(2, 2, 16 * 64, LANES),
-        ]
-        + [pltpu.VMEM(value.shape, value.dtype) for value in arguments]
-        + [pltpu.SemaphoreType.DMA((len(arguments),))],
-        [exchange(send, CHUNK, CHUNK)] + arguments,
-        [VMEM] + [hbm] * len(arguments),
+        ],
+        [exchange(send, CHUNK, CHUNK), col_mask] + handed,
     )
     received = exchange(send, BACK, 2)
     combined, sums = call(
@@ -563,10 +581,9 @@
             vm(2, 2, cols, LANES),
             vm(2, 2, 8 * cols, LANES),
             vm(2 * cols, LANES),
-            vm(64, LANES),
             vm(2, 2, 16 * cols, LANES),
         ],
-        [received, own, near, high, low],
+        [received, row_mask, own, near, high, low],
     )
     out = call(
         lambda *refs: norm_kernel(total_chans, *refs),

time: 44.2 us -> 43.7 us (0.989)
  Pallas kernels: 5.55 us -> 5.05 us
    pallas_call x4, Pallas kernels: 5.55 us -> 5.05 us  [call(): pl.pallas_call(kernel, out_shape=outs, in_specs=[place] * len(inputs), ou...]
where the time goes in v3:
time: 43.7 us; the launch traced here: 43.5 us
  blocking collectives  37.2 us (85%)
  Pallas kernels  5.05 us (12%)
  waiting for transfers between devices  0.83 us (2%)
  starting transfers between devices  0.47 us (1%)
    all_to_all x2, blocking collectives, exchange(): lax.all_to_all(pieces, ('sp', 'ch'), split_axis=0, concat_axis=0, tiled=T...  37.2 us
    pallas_call x4, Pallas kernels, call(): pl.pallas_call(kernel, out_shape=outs, in_specs=[place] * len(inputs), ou...  5.05 us
  transfers between devices with their start and end apart: 1, of which 1 were waited for; matrix products, arithmetic and copies ran while one was open for 0% of the time, Pallas kernels for 0%

profile of v3, /device:TPU:1, one launch (start us, length us, event | category | flops | bytes accessed | tf_op | source)
XLA Modules:
  0.0 43.5 jit_solution(7254772918313131293)
XLA Ops:
  0.0 1.3 %prep.1 = (bf16[1024,128]{1,0:T(8,128)(2,1)S(1)}, bf16[1024,64]{1,0:T(8,128)(2,1)S(1)}, bf16[1024,128]{1,0:T(8,128)(2,1)S(1)}, f32[4,8,64]{2,1,0:T(8,128)S(1)}, ...) custom-call(bf16[128,128]{1,0:T(8,128)(2,1)} %bitcast.19, ...), custom_call_target="tpu_custom_call" | custom-call | tf_op jit(solution)/shard_map/prep/pallas_call | solution.py:466
  1.3 22.7 %all_to_all.10 = bf16[128,1,8,128]{3,2,1,0:T(8,128)(2,1)S(1)} all-to-all(bf16[128,1,8,128]{3,2,1,0:T(8,128)(2,1)S(1)} %bitcast.17), channel_id=1, replica_groups=mesh['sp'=32,'ch'=4] {'sp','ch'}, dimensions={0} | all-to-all | bytes 524288 | tf_op jit(solution)/shard_map/all_to_all | solution.py:484
  24.0 1.4 %columns.1 = (bf16[768,128]{1,0:T(8,128)(2,1)S(1)}, f32[56,128]{1,0:T(8,128)S(1)}, f32[56,128]{1,0:T(8,128)S(1)}, bf16[256,512]{1,0:T(8,128)(2,1)S(1)}, bf16[256...) custom-call(bf16[1024,128]{1,0:T(8,128)(2,1)S(1)} %bitcast.15, ...), custom_call_target="tpu_custom_call" | custom-call | tf_op jit(solution)/shard_map/columns/pallas_call | solution.py:466
  25.4 14.5 %all_to_all.11 = bf16[128,3,2,128]{3,2,1,0:T(2,128)(2,1)S(1)} all-to-all(bf16[128,3,2,128]{3,2,1,0:T(2,128)(2,1)S(1)} %bitcast.18), channel_id=1, replica_groups=mesh['sp'=32,'ch'=4] {'sp','ch'}, dimensions={0} | all-to-all | bytes 393216 | tf_op jit(solution)/shard_map/all_to_all | solution.py:484
  39.9 1.7 %rows.1 = (f32[128,128]{1,0:T(8,128)S(1)}, f32[16,128]{1,0:T(8,128)S(1)}) custom-call(bf16[768,128]{1,0:T(8,128)(2,1)S(1)} %bitcast.16, bf16[1024,128]{1,0:T(8,128)(2,1)S(1)} %get-tuple-element.34.mask_ref, f32[56,128]{1,0:T(8,128)S(1)} %get-tuple-element.35.own_ref, f32[56,128]{1,0:T(8,128)S(1)} %get-tuple-element.36.near_ref, ...), custom_call_target="tpu_custom_call" | custom-call | tf_op jit(solution)/shard_map/rows/pallas_call | solution.py:466
  41.6 0.5 %collective-permute-start = (f32[16,128]{1,0:T(8,128)S(1)}, f32[16,128]{1,0:T(8,128)S(1)}, u32[]{:S(2)}, u32[]{:S(2)}) collective-permute-start(f32[16,128]{1,0:T(8,128)S(1)} %get-tuple-element.40.refs_1_), channel_id=1, source_target_pairs={{0,1},{1,0},{2,3},{3,2},{4,5},{5,4},{6,7},{7,6},{8,9},{9,8},{10,11... | collective-permute-start | bytes 24584 | tf_op jit(solution)/shard_map/ppermute | solution.py:478
  42.1 0.8 %collective-permute-done.refs_2_ = f32[16,128]{1,0:T(8,128)S(1)} collective-permute-done((f32[16,128]{1,0:T(8,128)S(1)}, f32[16,128]{1,0:T(8,128)S(1)}, u32[]{:S(2)}, u32[]{:S(2)}) %collective-permute-start) | collective-permute-done | bytes 8224 | tf_op jit(solution)/shard_map/ppermute | solution.py:478
  42.9 0.6 %norm.1 = bf16[128,128]{1,0:T(8,128)(2,1)} custom-call(f32[128,128]{1,0:T(8,128)S(1)} %get-tuple-element.39.refs_0_, f32[16,128]{1,0:T(8,128)S(1)} %get-tuple-element.40.refs_1_, f32[16,128]{1,0:T(8,128)S(1)} %collective-permute-done.refs_2_, f32[128,128]{1,0:T(8,128)S(1)} %get-tuple-element.41.refs_3_, f32[2,128,128]{2,1,0:T(8,128)S(1)} %get-tuple-element.42.refs_4_), custom_call_target="tpu_custom_call" | custom-call | tf_op jit(solution)/shard_map/norm/pallas_call | solution.py:466
Async XLA Ops:
  41.6 1.3 %collective-permute-start = (f32[16,128]{1,0:T(8,128)S(1)}, f32[16,128]{1,0:T(8,128)S(1)}, u32[]{:S(2)}, u32[]{:S(2)}) collective-permute-start(f32[16,128]{1,0:T(8,128)S(1)} %get-tuple-element.40.refs_1_), channel_id=1, source_target_pairs={{0,1},{1,0},{2,3},{3,2},{4,5},{5,4},{6,7},{7,6},{8,9},{9,8},{10,11... | collective-permute-start | bytes 24584 | tf_op jit(solution)/shard_map/ppermute | solution.py:478

commit v4 on v3

--- a/solution.py
+++ b/solution.py
@@ -59,7 +59,7 @@
     count, kept = 11, 7
     sources, send_ref, col_mask_ref, row_mask_ref = refs[:count], *refs[count : count + 3]
     handed = refs[count + 3 : count + 3 + kept]
-    scr, vec, near, packed, *own, arrived = refs[count + 3 + kept :]
+    scr, tile, vec, near, packed, *own, arrived = refs[count + 3 + kept :]
     loaded = (*own, *handed)
     copies = start_copies(sources, loaded, arrived)
     for j in range(64):
@@ -67,7 +67,7 @@
         lane = iota((16, LANES), 1)
         col_mask_ref[rows, :] = jnp.where(lane[:, 0:64] == j, 1.0, 0.0).astype(BF16)
         row_mask_ref[rows, :] = jnp.where(lane // 2 == j, 1.0, 0.0).astype(BF16)
-    for copy in copies:
+    for copy in copies[:8]:
         copy.wait()
     x_ref, cw_ref, cb_ref, pw_ref, dtw_ref, dtb_ref, rate_ref, skip_ref = loaded[:8]
     chans = cw_ref.shape[1]
@@ -101,11 +101,12 @@
             second, odd_b, preferred_element_type=F32
         )
 
-    third = pw_ref[2].astype(F32)
-    fourth = pw_ref[3].astype(F32)
-    rest = jnp.concatenate([third[0:8], fourth[0:8], third[8:40], fourth[8:40]], axis=0)
-    packed[0:40, :] = pack(pw_ref[0], rest[0:40].astype(BF16))
-    packed[40:80, :] = pack(pw_ref[1], rest[40:80].astype(BF16))
+    parts = [pw_ref[k].astype(F32) for k in range(4)]
+    first = [parts[k][0:8] for k in (2, 3, 0, 1)] + [parts[0][8:40], parts[1][8:24]]
+    second = [parts[1][24:40], parts[2][8:40], parts[3][8:40]]
+    packed[0:80, :] = pack(
+        jnp.concatenate(first, axis=0).astype(BF16), jnp.concatenate(second, axis=0).astype(BF16)
+    )
     packed[80:112, :] = pack(high[0:half], high[half:])
     packed[112:128, :] = pack(low[0:16], low[16:])
     packed[128:160, :] = pack(shared[0:half], shared[half:])
@@ -120,9 +121,13 @@
     scr[last : last + 1, :] = jnp.zeros((1, LANES), F32)
     slab = lax.axis_index("sp")
     for piece in range(CHUNK - X_ROWS):
-        row = packed[pl.ds(32 * piece + slab, 1), :]
-        scr[pl.ds(base + X_ROWS + piece, LANES, stride=CHUNK), :] = jnp.broadcast_to(row, (LANES, LANES))
-    send_ref[...] = scr[base : base + CHUNK * LANES, :].astype(BF16)
+        tile[X_ROWS + piece : X_ROWS + piece + 1, :] = packed[pl.ds(32 * piece + slab, 1), :]
+    chunks = scr[base : base + CHUNK * LANES, :].reshape(LANES, CHUNK, LANES)
+    is_x = iota((1, CHUNK, LANES), 1) < X_ROWS
+    chunks = jnp.where(is_x, chunks, tile[...][None])
+    send_ref[...] = chunks.reshape(CHUNK * LANES, LANES).astype(BF16)
+    for copy in copies[8:]:
+        copy.wait()
 
 
 def lane_rows(parts, columns, mask_ref, weights):
@@ -198,11 +203,12 @@
             dt_rows = ref[32 + 8 * way : 40 + 8 * way, :]
             column = []
             for row in range(2):
-                column += [jnp.zeros((40 * way, LANES), F32)] if way else []
+                column.append(jnp.zeros((16 + 8 * way, LANES), F32))
                 column.append(jnp.where(lane_row == row, dt_rows, 0.0))
-                column.append(jnp.zeros((LANES - 40 * way - 8, LANES), F32))
+                column += [] if way else [jnp.zeros((8, LANES), F32)]
             columns.append(jnp.concatenate(column, axis=0))
-    return halves(jnp.concatenate(columns, axis=1))
+    high, low = halves(jnp.concatenate(columns, axis=1))
+    return jnp.concatenate([high, low], axis=0)
 
 
 def column_kernel(
@@ -218,8 +224,7 @@
     send_ref,
     own_ref,
     near_ref,
-    high_ref,
-    low_ref,
+    steps_ref,
     gate_ref,
     affine_ref,
     flat_scr,
@@ -295,7 +300,7 @@
     chans = dtw_ref.shape[2]
     dup = spread(chans, 0) + spread(chans, 1)
     row_weights(dtw_ref, dtb_ref, rate_ref, skip_ref, own_ref, dup)
-    high_ref[...], low_ref[...] = step_weights((own_ref, near_ref))
+    steps_ref[...] = step_weights((own_ref, near_ref))
     gate_ref[...] = silu(gate_in_ref[...].astype(F32))
     pick = iota((LANES, LANES), 0) == iota((LANES, LANES), 1)
     for index, ref in enumerate((gain_ref, bias_ref)):
@@ -327,11 +332,12 @@
 
     nt = (((1,), (1,)), ((), ()))
     proj = lax.dot_general(values_b, proj_w[0:128], nt, preferred_element_type=F32)
-    proj = proj.astype(BF16).astype(F32)
+    proj = proj.astype(BF16)
+    low = proj[:, 0:16]
+    proj = proj.astype(F32)
     turned = lax.dot_general(proj_w[96:160], values_b, nt, preferred_element_type=F32)
     turned = turned.astype(BF16)
 
-    low = lax.dot_general(values_b, proj_w[80:96], nt, preferred_element_type=F32).astype(BF16)
     dt_rows = vec[16:32]
     second_half = iota((16, 256), 0) >= 8
     rates = []
@@ -380,8 +386,7 @@
     mask_ref,
     own_ref,
     near_ref,
-    high_ref,
-    low_ref,
+    steps_ref,
     comb_ref,
     sums_ref,
     scr,
@@ -399,8 +404,10 @@
         return scr[pl.ds(row, cols, stride=BACK), :]
 
     proj = [chunk_row(2), chunk_row(3)]
-    both = jnp.concatenate(proj, axis=1).astype(BF16)
-    low_rank = two_part_dot(both, high_ref[...], low_ref[...])
+    lane = iota((cols, LANES), 1)
+    both = jnp.where(lane < 32, proj[0], roll(proj[1], 32, 1))
+    both = both[:, 0:64].astype(BF16)
+    low_rank = two_part_dot(both, steps_ref[0:64, :], steps_ref[64:, :])
     vecs = (own_ref, near_ref)
     verticals = (chunk_row(0), chunk_row(4))
     values = (chunk_row(1), chunk_row(5))
@@ -421,7 +428,7 @@
     by_row = jnp.where(alike, 1.0, 0.0).astype(BF16)
 
     def expand(way, which, first):
-        top = 40 * way + 8 + 16 * which
+        top = 32 + 32 * way + 16 * which
         start = LANES * (first // 64)
         parts = turned[top : top + 16, start : start + LANES].astype(BF16)
         return lane_rows(parts, [(first + j) % 64 for j in range(8)], mask_ref, by_row)
@@ -535,6 +542,7 @@
         + [struct(value.shape, value.dtype) for value in arguments[4:]],
         [
             vm(CHUNK * (cols + 4), LANES),
+            vm(CHUNK, LANES),
             vm(2 * VEC_PAIRS, chans),
             vm(64, chans),
             vm(160, LANES),
@@ -544,15 +552,14 @@
         arguments,
         pl.BlockSpec(memory_space=pltpu.HBM),
     )
-    send, own, near, high, low, gate, affine = call(
+    send, own, near, steps, gate, affine = call(
         column_kernel,
         "columns",
         [
             struct((BACK * cols, LANES), BF16),
             struct((56, LANES), F32),
             struct((56, LANES), F32),
-            struct((2 * LANES, 4 * LANES), BF16),
-            struct((2 * LANES, 4 * LANES), BF16),
+            struct((LANES, 4 * LANES), BF16),
             struct((LANES, cols), F32),
             struct((2, LANES, cols), F32),
         ],
@@ -583,7 +590,7 @@
             vm(2 * cols, LANES),
             vm(2, 2, 16 * cols, LANES),
         ],
-        [received, row_mask, own, near, high, low],
+        [received, row_mask, own, near, steps],
     )
     out = call(
         lambda *refs: norm_kernel(total_chans, *refs),

time: 43.7 us -> 43.7 us (level)
  no operation moved by 1% of the time
where the time goes in v4:
time: 43.7 us; the launch traced here: 43.5 us
  blocking collectives  37.2 us (85%)
  Pallas kernels  4.99 us (11%)
  waiting for transfers between devices  0.83 us (2%)
  starting transfers between devices  0.48 us (1%)
    all_to_all x2, blocking collectives, exchange(): lax.all_to_all(pieces, ('sp', 'ch'), split_axis=0, concat_axis=0, tiled=T...  37.2 us
    pallas_call x4, Pallas kernels, call(): pl.pallas_call(kernel, out_shape=outs, in_specs=[place] * len(inputs), ou...  4.99 us
  transfers between devices with their start and end apart: 1, of which 1 were waited for; matrix products, arithmetic and copies ran while one was open for 0% of the time, Pallas kernels for 0%

profile of v4, /device:TPU:1, one launch (start us, length us, event | category | flops | bytes accessed | tf_op | source)
XLA Modules:
  0.0 43.5 jit_solution(10459357051719742160)
XLA Ops:
  0.0 1.2 %prep.1 = (bf16[1024,128]{1,0:T(8,128)(2,1)S(1)}, bf16[1024,64]{1,0:T(8,128)(2,1)S(1)}, bf16[1024,128]{1,0:T(8,128)(2,1)S(1)}, f32[4,8,64]{2,1,0:T(8,128)S(1)}, ...) custom-call(bf16[128,128]{1,0:T(8,128)(2,1)} %bitcast.19, ...), custom_call_target="tpu_custom_call" | custom-call | tf_op jit(solution)/shard_map/prep/pallas_call | solution.py:473
  1.2 22.7 %all_to_all.10 = bf16[128,1,8,128]{3,2,1,0:T(8,128)(2,1)S(1)} all-to-all(bf16[128,1,8,128]{3,2,1,0:T(8,128)(2,1)S(1)} %bitcast.17), channel_id=1, replica_groups=mesh['sp'=32,'ch'=4] {'sp','ch'}, dimensions={0} | all-to-all | bytes 524288 | tf_op jit(solution)/shard_map/all_to_all | solution.py:491
  23.9 1.4 %columns.1 = (bf16[768,128]{1,0:T(8,128)(2,1)S(1)}, f32[56,128]{1,0:T(8,128)S(1)}, f32[56,128]{1,0:T(8,128)S(1)}, bf16[128,512]{1,0:T(8,128)(2,1)S(1)}, f32[128,...) custom-call(bf16[1024,128]{1,0:T(8,128)(2,1)S(1)} %bitcast.15, bf16[1024,64]{1,0:T(8,128)(2,1)S(1)} %get-tuple-element.24.mask_ref, ...), custom_call_target="tpu_custom_call" | custom-call | tf_op jit(solution)/shard_map/columns/pallas_call | solution.py:473
  25.3 14.5 %all_to_all.11 = bf16[128,3,2,128]{3,2,1,0:T(2,128)(2,1)S(1)} all-to-all(bf16[128,3,2,128]{3,2,1,0:T(2,128)(2,1)S(1)} %bitcast.18), channel_id=1, replica_groups=mesh['sp'=32,'ch'=4] {'sp','ch'}, dimensions={0} | all-to-all | bytes 393216 | tf_op jit(solution)/shard_map/all_to_all | solution.py:491
  39.8 1.7 %rows.1 = (f32[128,128]{1,0:T(8,128)S(1)}, f32[16,128]{1,0:T(8,128)S(1)}) custom-call(bf16[768,128]{1,0:T(8,128)(2,1)S(1)} %bitcast.16, bf16[1024,128]{1,0:T(8,128)(2,1)S(1)} %get-tuple-element.33.mask_ref, f32[56,128]{1,0:T(8,128)S(1)} %get-tuple-element.34.own_ref, f32[56,128]{1,0:T(8,128)S(1)} %get-tuple-element.35.near_ref, ...), custom_call_target="tpu_custom_call" | custom-call | tf_op jit(solution)/shard_map/rows/pallas_call | solution.py:473
  41.5 0.5 %collective-permute-start = (f32[16,128]{1,0:T(8,128)S(1)}, f32[16,128]{1,0:T(8,128)S(1)}, u32[]{:S(2)}, u32[]{:S(2)}) collective-permute-start(f32[16,128]{1,0:T(8,128)S(1)} %get-tuple-element.38.refs_1_), channel_id=1, source_target_pairs={{0,1},{1,0},{2,3},{3,2},{4,5},{5,4},{6,7},{7,6},{8,9},{9,8},{10,11... | collective-permute-start | bytes 24584 | tf_op jit(solution)/shard_map/ppermute | solution.py:485
  42.0 0.8 %collective-permute-done.refs_2_ = f32[16,128]{1,0:T(8,128)S(1)} collective-permute-done((f32[16,128]{1,0:T(8,128)S(1)}, f32[16,128]{1,0:T(8,128)S(1)}, u32[]{:S(2)}, u32[]{:S(2)}) %collective-permute-start) | collective-permute-done | bytes 8224 | tf_op jit(solution)/shard_map/ppermute | solution.py:485
  42.8 0.6 %norm.1 = bf16[128,128]{1,0:T(8,128)(2,1)} custom-call(f32[128,128]{1,0:T(8,128)S(1)} %get-tuple-element.37.refs_0_, f32[16,128]{1,0:T(8,128)S(1)} %get-tuple-element.38.refs_1_, f32[16,128]{1,0:T(8,128)S(1)} %collective-permute-done.refs_2_, f32[128,128]{1,0:T(8,128)S(1)} %get-tuple-element.39.refs_3_, f32[2,128,128]{2,1,0:T(8,128)S(1)} %get-tuple-element.40.refs_4_), custom_call_target="tpu_custom_call" | custom-call | tf_op jit(solution)/shard_map/norm/pallas_call | solution.py:473
Async XLA Ops:
  41.5 1.3 %collective-permute-start = (f32[16,128]{1,0:T(8,128)S(1)}, f32[16,128]{1,0:T(8,128)S(1)}, u32[]{:S(2)}, u32[]{:S(2)}) collective-permute-start(f32[16,128]{1,0:T(8,128)S(1)} %get-tuple-element.38.refs_1_), channel_id=1, source_target_pairs={{0,1},{1,0},{2,3},{3,2},{4,5},{5,4},{6,7},{7,6},{8,9},{9,8},{10,11... | collective-permute-start | bytes 24584 | tf_op jit(solution)/shard_map/ppermute | solution.py:485

commit v5 on v4

--- a/solution.py
+++ b/solution.py
@@ -218,15 +218,10 @@
     dtb_ref,
     rate_ref,
     skip_ref,
-    gain_ref,
-    bias_ref,
-    gate_in_ref,
     send_ref,
     own_ref,
     near_ref,
     steps_ref,
-    gate_ref,
-    affine_ref,
     flat_scr,
     back_scr,
     scr,
@@ -301,11 +296,6 @@
     dup = spread(chans, 0) + spread(chans, 1)
     row_weights(dtw_ref, dtb_ref, rate_ref, skip_ref, own_ref, dup)
     steps_ref[...] = step_weights((own_ref, near_ref))
-    gate_ref[...] = silu(gate_in_ref[...].astype(F32))
-    pick = iota((LANES, LANES), 0) == iota((LANES, LANES), 1)
-    for index, ref in enumerate((gain_ref, bias_ref)):
-        column = jnp.sum(jnp.where(pick, dup_rows(ref[...], dup), 0.0), axis=1, keepdims=True)
-        affine_ref[index] = jnp.broadcast_to(column, (LANES, LANES))
 
     def from_even(left, right):
         mask = iota(left.shape, 1) % 2 == 0
@@ -453,7 +443,16 @@
         sums_ref[8 * index : 8 * index + 8, :] = value
 
 
-def norm_kernel(total_chans, comb_ref, s0_ref, s1_ref, gate_ref, affine_ref, out_ref):
+def gate_kernel(sums_ref, gain_ref, bias_ref, gate_in_ref, affine_ref):
+    chans = gain_ref.shape[1]
+    gate = silu(gate_in_ref[...].astype(F32))
+    pick = iota((LANES, chans), 0) // 2 == iota((LANES, chans), 1)
+    for index, ref in enumerate((gain_ref, bias_ref)):
+        column = jnp.sum(jnp.where(pick, ref[...], 0.0), axis=1, keepdims=True)
+        affine_ref[index] = column * gate
+
+
+def norm_kernel(total_chans, comb_ref, s0_ref, s1_ref, affine_ref, out_ref):
     sums = s0_ref[...] + s1_ref[...]
     mean = sums[0:8] / total_chans
     var = sums[8:16] / total_chans - mean * mean
@@ -461,8 +460,7 @@
     comb = comb_ref[...]
     means = jnp.concatenate([mean] * (LANES // 8), axis=0)
     scales = jnp.concatenate([scale] * (LANES // 8), axis=0)
-    normed = (comb - means) * scales * affine_ref[0] + affine_ref[1]
-    out_ref[...] = (normed * gate_ref[...]).astype(BF16)
+    out_ref[...] = ((comb - means) * scales * affine_ref[0] + affine_ref[1]).astype(BF16)
 
 
 VMEM = pl.BlockSpec(memory_space=pltpu.VMEM)
@@ -552,7 +550,7 @@
         arguments,
         pl.BlockSpec(memory_space=pltpu.HBM),
     )
-    send, own, near, steps, gate, affine = call(
+    send, own, near, steps = call(
         column_kernel,
         "columns",
         [
@@ -560,8 +558,6 @@
             struct((56, LANES), F32),
             struct((56, LANES), F32),
             struct((LANES, 4 * LANES), BF16),
-            struct((LANES, cols), F32),
-            struct((2, LANES, cols), F32),
         ],
         [
             vm(CHUNK * cols, LANES),
@@ -574,7 +570,7 @@
             vm(LANES, LANES),
             vm(2, 2, 16 * 64, LANES),
         ],
-        [exchange(send, CHUNK, CHUNK), col_mask] + handed,
+        [exchange(send, CHUNK, CHUNK), col_mask] + handed[:4],
     )
     received = exchange(send, BACK, 2)
     combined, sums = call(
@@ -592,12 +588,15 @@
         ],
         [received, row_mask, own, near, steps],
     )
+    affine = call(
+        gate_kernel, "gate", struct((2, LANES, cols), F32), [], [sums] + handed[4:]
+    )
     out = call(
         lambda *refs: norm_kernel(total_chans, *refs),
         "norm",
         struct(flat, BF16),
         [],
-        [combined, sums, other(sums, 1), gate, affine],
+        [combined, sums, other(sums, 1), affine],
     )
     return out.reshape(chans, rows, cols)
 

time: 43.7 us -> 43.6 us (level)
    pallas_call x4 -> x5, Pallas kernels: 4.99 us -> 5.05 us  [call(): pl.pallas_call(kernel, out_shape=outs, in_specs=[place] * len(inputs), ou...]
where the time goes in v5:
time: 43.6 us; the launch traced here: 43.4 us
  blocking collectives  37.2 us (85%)
  Pallas kernels  5.05 us (12%)
  waiting for transfers between devices  0.71 us (2%)
  starting transfers between devices  0.48 us (1%)
    all_to_all x2, blocking collectives, exchange(): lax.all_to_all(pieces, ('sp', 'ch'), split_axis=0, concat_axis=0, tiled=T...  37.2 us
    pallas_call x5, Pallas kernels, call(): pl.pallas_call(kernel, out_shape=outs, in_specs=[place] * len(inputs), ou...  5.05 us
  transfers between devices with their start and end apart: 1, of which 1 were waited for; matrix products, arithmetic and copies ran while one was open for 0% of the time, Pallas kernels for 0%

profile of v5, /device:TPU:1, one launch (start us, length us, event | category | flops | bytes accessed | tf_op | source)
XLA Modules:
  0.0 43.4 jit_solution(824815585270417702)
XLA Ops:
  0.0 1.2 %prep.1 = (bf16[1024,128]{1,0:T(8,128)(2,1)S(1)}, bf16[1024,64]{1,0:T(8,128)(2,1)S(1)}, bf16[1024,128]{1,0:T(8,128)(2,1)S(1)}, f32[4,8,64]{2,1,0:T(8,128)S(1)}, ...) custom-call(bf16[128,128]{1,0:T(8,128)(2,1)} %bitcast.19, ...), custom_call_target="tpu_custom_call" | custom-call | tf_op jit(solution)/shard_map/prep/pallas_call | solution.py:471
  1.2 22.7 %all_to_all.10 = bf16[128,1,8,128]{3,2,1,0:T(8,128)(2,1)S(1)} all-to-all(bf16[128,1,8,128]{3,2,1,0:T(8,128)(2,1)S(1)} %bitcast.17), channel_id=1, replica_groups=mesh['sp'=32,'ch'=4] {'sp','ch'}, dimensions={0} | all-to-all | bytes 524288 | tf_op jit(solution)/shard_map/all_to_all | solution.py:489
  23.9 1.4 %columns.1 = (bf16[768,128]{1,0:T(8,128)(2,1)S(1)}, f32[56,128]{1,0:T(8,128)S(1)}, f32[56,128]{1,0:T(8,128)S(1)}, bf16[128,512]{1,0:T(8,128)(2,1)S(1)}) custom-call(bf16[1024,128]{1,0:T(8,128)(2,1)S(1)} %bitcast.15, bf16[1024,64]{1,0:T(8,128)(2,1)S(1)} %get-tuple-element.22.mask_ref, f32[4,8,64]{2,1,0:T(8,128)S(1)} %get-tuple-element.23.dtw_ref, ...), custom_call_target="tpu_custom_call" | custom-call | tf_op jit(solution)/shard_map/columns/pallas_call | solution.py:471
  25.3 14.5 %all_to_all.11 = bf16[128,3,2,128]{3,2,1,0:T(2,128)(2,1)S(1)} all-to-all(bf16[128,3,2,128]{3,2,1,0:T(2,128)(2,1)S(1)} %bitcast.18), channel_id=1, replica_groups=mesh['sp'=32,'ch'=4] {'sp','ch'}, dimensions={0} | all-to-all | bytes 393216 | tf_op jit(solution)/shard_map/all_to_all | solution.py:489
  39.7 1.7 %rows.1 = (f32[128,128]{1,0:T(8,128)S(1)}, f32[16,128]{1,0:T(8,128)S(1)}) custom-call(bf16[768,128]{1,0:T(8,128)(2,1)S(1)} %bitcast.16, bf16[1024,128]{1,0:T(8,128)(2,1)S(1)} %get-tuple-element.28.mask_ref, f32[56,128]{1,0:T(8,128)S(1)} %get-tuple-element.29.own_ref, f32[56,128]{1,0:T(8,128)S(1)} %get-tuple-element.30.near_ref, ...), custom_call_target="tpu_custom_call" | custom-call | tf_op jit(solution)/shard_map/rows/pallas_call | solution.py:471
  41.5 0.5 %collective-permute-start = (f32[16,128]{1,0:T(8,128)S(1)}, f32[16,128]{1,0:T(8,128)S(1)}, u32[]{:S(2)}, u32[]{:S(2)}) collective-permute-start(f32[16,128]{1,0:T(8,128)S(1)} %get-tuple-element.33.sums_ref.refs_1_), channel_id=1, source_target_pairs={{0,1},{1,0},{2,3},{3,2},{4,5},{5,4},{6,7},{7,6},{8,9},{9,8},{10,11... | collective-permute-start | bytes 24584 | tf_op jit(solution)/shard_map/ppermute | solution.py:483
  42.0 0.1 gate.1.refs_3_
  42.1 0.7 %collective-permute-done.refs_2_ = f32[16,128]{1,0:T(8,128)S(1)} collective-permute-done((f32[16,128]{1,0:T(8,128)S(1)}, f32[16,128]{1,0:T(8,128)S(1)}, u32[]{:S(2)}, u32[]{:S(2)}) %collective-permute-start) | collective-permute-done | bytes 8224 | tf_op jit(solution)/shard_map/ppermute | solution.py:483
  42.8 0.6 %norm.1 = bf16[128,128]{1,0:T(8,128)(2,1)} custom-call(f32[128,128]{1,0:T(8,128)S(1)} %get-tuple-element.32.refs_0_, f32[16,128]{1,0:T(8,128)S(1)} %get-tuple-element.33.sums_ref.refs_1_, f32[16,128]{1,0:T(8,128)S(1)} %collective-permute-done.refs_2_, f32[2,128,128]{2,1,0:T(8,128)S(1)} %gate.1.refs_3_), custom_call_target="tpu_custom_call" | custom-call | tf_op jit(solution)/shard_map/norm/pallas_call | solution.py:471
Async XLA Ops:
  41.5 1.3 %collective-permute-start = (f32[16,128]{1,0:T(8,128)S(1)}, f32[16,128]{1,0:T(8,128)S(1)}, u32[]{:S(2)}, u32[]{:S(2)}) collective-permute-start(f32[16,128]{1,0:T(8,128)S(1)} %get-tuple-element.33.sums_ref.refs_1_), channel_id=1, source_target_pairs={{0,1},{1,0},{2,3},{3,2},{4,5},{5,4},{6,7},{7,6},{8,9},{9,8},{10,11... | collective-permute-start | bytes 24584 | tf_op jit(solution)/shard_map/ppermute | solution.py:483

commit v6 on v5

--- a/solution.py
+++ b/solution.py
@@ -130,9 +130,10 @@
         copy.wait()
 
 
-def lane_rows(parts, columns, mask_ref, weights):
-    picked = [parts * mask_ref[16 * j : 16 * j + 16, :] for j in columns]
-    return jnp.dot(jnp.concatenate(picked, axis=0), weights, preferred_element_type=F32)
+def lane_rows(pieces, columns, mask_ref, weights):
+    picked = [parts * mask_ref[16 * j : 16 * j + 16, :] for parts in pieces for j in columns]
+    wide = jnp.dot(jnp.concatenate(picked, axis=0), weights, preferred_element_type=F32)
+    return wide.reshape(len(pieces), LANES, LANES)
 
 
 def scan_pair(steps, rates, delta_ref, drive_ref, expand, wide_ref, part_ref, row_of):
@@ -142,8 +143,9 @@
     def prepare(turn):
         for way in range(2):
             first = 8 * turn if way == 0 else steps - 8 - 8 * turn
+            wide = expand(way, first)
             for which in range(2):
-                wide_ref[way, which, 16 * first : 16 * first + LANES, :] = expand(way, which, first)
+                wide_ref[way, which, 16 * first : 16 * first + LANES, :] = wide[which]
 
     prepare(0)
     for step in range(steps):
@@ -347,9 +349,9 @@
 
     ones = jnp.ones((64, LANES), BF16)
 
-    def expand(way, which, first):
-        parts = turned[32 * way + 16 * which : 32 * way + 16 * which + 16]
-        return lane_rows(parts, [row_of(first + j) for j in range(8)], mask_ref, ones)
+    def expand(way, first):
+        tops = (32 * way, 32 * way + 16)
+        return lane_rows([turned[top : top + 16] for top in tops], [row_of(first + j) for j in range(8)], mask_ref, ones)
 
     scan_pair(2 * slabs, rates, delta_scr, drive_scr, expand, wide_scr, part_scr, row_of)
 
@@ -417,10 +419,10 @@
     alike = iota((LANES, LANES), 0) % 2 == iota((LANES, LANES), 1) % 2
     by_row = jnp.where(alike, 1.0, 0.0).astype(BF16)
 
-    def expand(way, which, first):
-        top = 32 + 32 * way + 16 * which
+    def expand(way, first):
         start = LANES * (first // 64)
-        parts = turned[top : top + 16, start : start + LANES].astype(BF16)
+        tops = (32 + 32 * way, 48 + 32 * way)
+        parts = [turned[top : top + 16, start : start + LANES].astype(BF16) for top in tops]
         return lane_rows(parts, [(first + j) % 64 for j in range(8)], mask_ref, by_row)
 
     scan_pair(cols, rates, delta_scr, drive_scr, expand, wide_scr, part_scr, lambda at: at)

time: 43.6 us -> 43.6 us (level)
  no operation moved by 1% of the time
where the time goes in v6:
time: 43.6 us; the launch traced here: 43.4 us
  blocking collectives  37.2 us (85%)
  Pallas kernels  4.99 us (11%)
  waiting for transfers between devices  0.71 us (2%)
  starting transfers between devices  0.47 us (1%)
    all_to_all x2, blocking collectives, exchange(): lax.all_to_all(pieces, ('sp', 'ch'), split_axis=0, concat_axis=0, tiled=T...  37.2 us
    pallas_call x5, Pallas kernels, call(): pl.pallas_call(kernel, out_shape=outs, in_specs=[place] * len(inputs), ou...  4.99 us
  transfers between devices with their start and end apart: 1, of which 1 were waited for; matrix products, arithmetic and copies ran while one was open for 0% of the time, Pallas kernels for 0%

profile of v6, /device:TPU:1, one launch (start us, length us, event | category | flops | bytes accessed | tf_op | source)
XLA Modules:
  0.0 43.4 jit_solution(8391591349992861620)
XLA Ops:
  0.0 1.2 %prep.1 = (bf16[1024,128]{1,0:T(8,128)(2,1)S(1)}, bf16[1024,64]{1,0:T(8,128)(2,1)S(1)}, bf16[1024,128]{1,0:T(8,128)(2,1)S(1)}, f32[4,8,64]{2,1,0:T(8,128)S(1)}, ...) custom-call(bf16[128,128]{1,0:T(8,128)(2,1)} %bitcast.19, ...), custom_call_target="tpu_custom_call" | custom-call | tf_op jit(solution)/shard_map/prep/pallas_call | solution.py:473
  1.2 22.7 %all_to_all.10 = bf16[128,1,8,128]{3,2,1,0:T(8,128)(2,1)S(1)} all-to-all(bf16[128,1,8,128]{3,2,1,0:T(8,128)(2,1)S(1)} %bitcast.17), channel_id=1, replica_groups=mesh['sp'=32,'ch'=4] {'sp','ch'}, dimensions={0} | all-to-all | bytes 524288 | tf_op jit(solution)/shard_map/all_to_all | solution.py:491
  23.9 1.3 %columns.1 = (bf16[768,128]{1,0:T(8,128)(2,1)S(1)}, f32[56,128]{1,0:T(8,128)S(1)}, f32[56,128]{1,0:T(8,128)S(1)}, bf16[128,512]{1,0:T(8,128)(2,1)S(1)}) custom-call(bf16[1024,128]{1,0:T(8,128)(2,1)S(1)} %bitcast.15, bf16[1024,64]{1,0:T(8,128)(2,1)S(1)} %get-tuple-element.22.mask_ref, f32[4,8,64]{2,1,0:T(8,128)S(1)} %get-tuple-element.23.dtw_ref, ...), custom_call_target="tpu_custom_call" | custom-call | tf_op jit(solution)/shard_map/columns/pallas_call | solution.py:473
  25.2 14.5 %all_to_all.11 = bf16[128,3,2,128]{3,2,1,0:T(2,128)(2,1)S(1)} all-to-all(bf16[128,3,2,128]{3,2,1,0:T(2,128)(2,1)S(1)} %bitcast.18), channel_id=1, replica_groups=mesh['sp'=32,'ch'=4] {'sp','ch'}, dimensions={0} | all-to-all | bytes 393216 | tf_op jit(solution)/shard_map/all_to_all | solution.py:491
  39.7 1.7 %rows.1 = (f32[128,128]{1,0:T(8,128)S(1)}, f32[16,128]{1,0:T(8,128)S(1)}) custom-call(bf16[768,128]{1,0:T(8,128)(2,1)S(1)} %bitcast.16, bf16[1024,128]{1,0:T(8,128)(2,1)S(1)} %get-tuple-element.28.mask_ref, f32[56,128]{1,0:T(8,128)S(1)} %get-tuple-element.29.own_ref, f32[56,128]{1,0:T(8,128)S(1)} %get-tuple-element.30.near_ref, ...), custom_call_target="tpu_custom_call" | custom-call | tf_op jit(solution)/shard_map/rows/pallas_call | solution.py:473
  41.4 0.5 %collective-permute-start = (f32[16,128]{1,0:T(8,128)S(1)}, f32[16,128]{1,0:T(8,128)S(1)}, u32[]{:S(2)}, u32[]{:S(2)}) collective-permute-start(f32[16,128]{1,0:T(8,128)S(1)} %get-tuple-element.33.sums_ref.refs_1_), channel_id=1, source_target_pairs={{0,1},{1,0},{2,3},{3,2},{4,5},{5,4},{6,7},{7,6},{8,9},{9,8},{10,11... | collective-permute-start | bytes 24584 | tf_op jit(solution)/shard_map/ppermute | solution.py:485
  41.9 0.1 gate.1.refs_3_
  42.0 0.7 %collective-permute-done.refs_2_ = f32[16,128]{1,0:T(8,128)S(1)} collective-permute-done((f32[16,128]{1,0:T(8,128)S(1)}, f32[16,128]{1,0:T(8,128)S(1)}, u32[]{:S(2)}, u32[]{:S(2)}) %collective-permute-start) | collective-permute-done | bytes 8224 | tf_op jit(solution)/shard_map/ppermute | solution.py:485
  42.7 0.6 %norm.1 = bf16[128,128]{1,0:T(8,128)(2,1)} custom-call(f32[128,128]{1,0:T(8,128)S(1)} %get-tuple-element.32.refs_0_, f32[16,128]{1,0:T(8,128)S(1)} %get-tuple-element.33.sums_ref.refs_1_, f32[16,128]{1,0:T(8,128)S(1)} %collective-permute-done.refs_2_, f32[2,128,128]{2,1,0:T(8,128)S(1)} %gate.1.refs_3_), custom_call_target="tpu_custom_call" | custom-call | tf_op jit(solution)/shard_map/norm/pallas_call | solution.py:473
Async XLA Ops:
  41.4 1.3 %collective-permute-start = (f32[16,128]{1,0:T(8,128)S(1)}, f32[16,128]{1,0:T(8,128)S(1)}, u32[]{:S(2)}, u32[]{:S(2)}) collective-permute-start(f32[16,128]{1,0:T(8,128)S(1)} %get-tuple-element.33.sums_ref.refs_1_), channel_id=1, source_target_pairs={{0,1},{1,0},{2,3},{3,2},{4,5},{5,4},{6,7},{7,6},{8,9},{9,8},{10,11... | collective-permute-start | bytes 24584 | tf_op jit(solution)/shard_map/ppermute | solution.py:485
